TPU v7x, 32 devices: a whole 2x2x4 slice. The times are simulated.
32 devices in a mesh: cuts: 1, state: 32 (over z, y, x, core).
Axes of the slice: x: 2, y: 2, z: 4, core: 2. Of those that a mesh axis runs over, the one named last changes fastest.
Arguments:
- initial_states: bfloat16 [256, 32, 48, 128], P(('cuts', 'state')), may hold values from -36 to 36
- potential: float32 [32, 48, 128], replicated, may hold values from -1 to 0
- bounds: int32 [2], P('cuts'), may hold values from -32 to 159, as said below
Outputs:
- orthonormal: float32 [256, 196608], P('cuts', 'state')
Inputs may be any that keep to these rules, and one draw needn't show every extreme that they name: `bounds`: the first entry lies in -32 to -17, inside the spectrum of H, and the second in 136 to 159, above it; the anchor -1.125 lies below the spectrum.
All inputs are finite; a program needn't handle non-finite values.
Results may differ from a plain program's by a relative error of at most 0.0003.
Values sent between devices are 32-bit elements; how exact they have to be, the bound alone decides.
No kernel may reach another device: no remote copies, remote signals or barrier semaphores. Data moves between devices by JAX's collectives and lax.ppermute only.
A program may use at most 192 MiB of HBM per device.

v0:
```python
import math

import jax
import jax.numpy as jnp
from jax import lax
from jax.sharding import PartitionSpec as P

DEGREE = 16


STENCIL_NEAR = 4.0 / 3.0
STENCIL_FAR = -1.0 / 12.0
STENCIL_SELF = -5.0 / 2.0
ANCHOR_VALUE = -1.125


def laplace_periodic(values, axis_dim):
    near_sum = jnp.roll(values, 1, axis_dim) + jnp.roll(values, -1, axis_dim)
    far_sum = jnp.roll(values, 2, axis_dim) + jnp.roll(values, -2, axis_dim)
    return STENCIL_NEAR * near_sum + STENCIL_FAR * far_sum


def laplace_walled(values):
    extent = values.shape[1]
    padded = jnp.pad(values, ((0, 0), (2, 2), (0, 0), (0, 0)))
    near_sum = padded[:, 1 : extent + 1] + padded[:, 3 : extent + 3]
    far_sum = padded[:, 0:extent] + padded[:, 4 : extent + 4]
    return STENCIL_NEAR * near_sum + STENCIL_FAR * far_sum


def apply_hamiltonian(values, potential):
    laplace = 3.0 * STENCIL_SELF * values + laplace_walled(values)
    laplace = laplace + laplace_periodic(values, 2) + laplace_periodic(values, 3)
    return -0.5 * laplace + potential[None] * values


def filter_states(states, potential, bounds):
    low_end = bounds[0].astype(jnp.float32) / 64.0
    high_end = bounds[1].astype(jnp.float32) / 16.0
    half_width = (high_end - low_end) / 2.0
    centre = (high_end + low_end) / 2.0
    sigma_now = half_width / (ANCHOR_VALUE - centre)
    tau_value = 2.0 / sigma_now
    current = (apply_hamiltonian(states, potential) - centre * states) * (sigma_now / half_width)

    def degree_step(degree, carried):
        previous, current, sigma_now = carried
        sigma_next = 1.0 / (tau_value - sigma_now)
        latest = (apply_hamiltonian(current, potential) - centre * current) * (
            2.0 * sigma_next / half_width
        )
        latest = latest - sigma_now * sigma_next * previous
        return (current, latest, sigma_next)

    carried = lax.fori_loop(1, DEGREE, degree_step, (states, current, sigma_now))
    return carried[1]


def outer_product(left, right):
    return lax.dot_general(
        left,
        right,
        (((1,), (1,)), ((), ())),
        precision=lax.Precision.HIGHEST,
        preferred_element_type=jnp.float32,
    )


def per_device(initial_states, potential, bounds):
    filtered = filter_states(initial_states.astype(jnp.float32), potential, bounds)
    points = filtered.shape[1] * filtered.shape[2] * filtered.shape[3]
    flat = filtered.reshape(filtered.shape[0], points)
    row_block = lax.all_to_all(flat, "state", split_axis=1, concat_axis=0, tiled=True)
    gram_local = outer_product(row_block, row_block)
    gram_total = lax.psum(gram_local, "state")
    factor = jnp.linalg.cholesky(gram_total)
    solved = lax.linalg.triangular_solve(factor, row_block, left_side=True, lower=True)
    return solved * math.sqrt(points)


def solution(mesh):
    return jax.shard_map(
        per_device,
        mesh=mesh,
        in_specs=(P(("cuts", "state"), None, None, None), P(), P("cuts")),
        out_specs=P("cuts", "state"),
        check_vma=False,
    )
```

profile of v0, /device:TPU:0, one launch (start us, length us, event | category | flops | bytes accessed | tf_op | source)
XLA Modules:
  0.0 1869.4 jit_solution(1136967705735163389)
XLA Ops:
  50.8 37.2 %fusion.28 = f32[8,32,48,128]{3,2,1,0:T(8,128)} fusion(f32[8,32,48,128]{3,2,1,0:T(8,128)} %convert_element_type.16, f32[8,32,47,128]{3,2,1,0:T(8,128)} %get-tuple-element.170, f32[8,32,1,128]{3,2,1,0:T(1,128)S(1)} %get-tuple-element.172, f32[8,32,1,128]{3,2,1,0:T(1,128)S(1)} %get-tuple-element.171, f32[8,32,47,128]{3,2,1,0:T(8,128)} %get-tuple-element.169, ...), kind=kLoop, calls=%fused_computation.43 | loop fusion | flops 51904512 | bytes 63701000 | tf_op jit(solution)/shard_map/mul | solution.py:44
  87.9 1411.8 %while.17 = (s32[]{:T(128)}, f32[8,32,48,128]{3,2,1,0:T(8,128)}, f32[8,32,48,128]{3,2,1,0:T(8,128)}, f32[]{:T(128)}, f32[32,48,128]{2,1,0:T(8,128)S(1)}, /*index...) while((s32[]{:T(128)}, f32[8,32,48,128]{3,2,1,0:T(8,128)}, ...), condition=%wide.region_1.2_spmd, body=%wide.region_0.1_spmd.sunk | while | flops 55050248 | bytes 243007824 | solution.py:55
  88.0 10.6 fusion.78
  132.7 39.8 %fusion.86 = f32[8,32,48,128]{3,2,1,0:T(8,128)} fusion(f32[8,32,48,128]{3,2,1,0:T(8,128)} %get-tuple-element.306, f32[8,32,47,128]{3,2,1,0:T(8,128)} %get-tuple-element.271, f32[8,32,1,128]{3,2,1,0:T(1,128)} %get-tuple-element.272, f32[8,32,1,128]{3,2,1,0:T(1,128)S(1)} %get-tuple-element.273, f32[8,32,47,128]{3,2,1,0:T(8,128)} %get-tuple-element.274, ...), kind=kLoop, calls=%fused_computation.14.clone.1 | loop fusion | flops 55050240 | bytes 69992464 | tf_op jit(solution)/shard_map/while/body/eval_jaxpr/sub | solution.py:52
  181.4 10.6 fusion.78
  226.1 39.8 %fusion.86 = f32[8,32,48,128]{3,2,1,0:T(8,128)} fusion(f32[8,32,48,128]{3,2,1,0:T(8,128)} %get-tuple-element.306, f32[8,32,47,128]{3,2,1,0:T(8,128)} %get-tuple-element.271, f32[8,32,1,128]{3,2,1,0:T(1,128)} %get-tuple-element.272, f32[8,32,1,128]{3,2,1,0:T(1,128)S(1)} %get-tuple-element.273, f32[8,32,47,128]{3,2,1,0:T(8,128)} %get-tuple-element.274, ...), kind=kLoop, calls=%fused_computation.14.clone.1 | loop fusion | flops 55050240 | bytes 69992464 | tf_op jit(solution)/shard_map/while/body/eval_jaxpr/sub | solution.py:52
  274.7 10.6 fusion.78
  319.5 39.8 %fusion.86 = f32[8,32,48,128]{3,2,1,0:T(8,128)} fusion(f32[8,32,48,128]{3,2,1,0:T(8,128)} %get-tuple-element.306, f32[8,32,47,128]{3,2,1,0:T(8,128)} %get-tuple-element.271, f32[8,32,1,128]{3,2,1,0:T(1,128)} %get-tuple-element.272, f32[8,32,1,128]{3,2,1,0:T(1,128)S(1)} %get-tuple-element.273, f32[8,32,47,128]{3,2,1,0:T(8,128)} %get-tuple-element.274, ...), kind=kLoop, calls=%fused_computation.14.clone.1 | loop fusion | flops 55050240 | bytes 69992464 | tf_op jit(solution)/shard_map/while/body/eval_jaxpr/sub | solution.py:52
  412.8 39.8 %fusion.86 = f32[8,32,48,128]{3,2,1,0:T(8,128)} fusion(f32[8,32,48,128]{3,2,1,0:T(8,128)} %get-tuple-element.306, f32[8,32,47,128]{3,2,1,0:T(8,128)} %get-tuple-element.271, f32[8,32,1,128]{3,2,1,0:T(1,128)} %get-tuple-element.272, f32[8,32,1,128]{3,2,1,0:T(1,128)S(1)} %get-tuple-element.273, f32[8,32,47,128]{3,2,1,0:T(8,128)} %get-tuple-element.274, ...), kind=kLoop, calls=%fused_computation.14.clone.1 | loop fusion | flops 55050240 | bytes 69992464 | tf_op jit(solution)/shard_map/while/body/eval_jaxpr/sub | solution.py:52
  461.5 10.6 fusion.78
  506.2 39.8 %fusion.86 = f32[8,32,48,128]{3,2,1,0:T(8,128)} fusion(f32[8,32,48,128]{3,2,1,0:T(8,128)} %get-tuple-element.306, f32[8,32,47,128]{3,2,1,0:T(8,128)} %get-tuple-element.271, f32[8,32,1,128]{3,2,1,0:T(1,128)} %get-tuple-element.272, f32[8,32,1,128]{3,2,1,0:T(1,128)S(1)} %get-tuple-element.273, f32[8,32,47,128]{3,2,1,0:T(8,128)} %get-tuple-element.274, ...), kind=kLoop, calls=%fused_computation.14.clone.1 | loop fusion | flops 55050240 | bytes 69992464 | tf_op jit(solution)/shard_map/while/body/eval_jaxpr/sub | solution.py:52
  599.6 39.8 %fusion.86 = f32[8,32,48,128]{3,2,1,0:T(8,128)} fusion(f32[8,32,48,128]{3,2,1,0:T(8,128)} %get-tuple-element.306, f32[8,32,47,128]{3,2,1,0:T(8,128)} %get-tuple-element.271, f32[8,32,1,128]{3,2,1,0:T(1,128)} %get-tuple-element.272, f32[8,32,1,128]{3,2,1,0:T(1,128)S(1)} %get-tuple-element.273, f32[8,32,47,128]{3,2,1,0:T(8,128)} %get-tuple-element.274, ...), kind=kLoop, calls=%fused_computation.14.clone.1 | loop fusion | flops 55050240 | bytes 69992464 | tf_op jit(solution)/shard_map/while/body/eval_jaxpr/sub | solution.py:52
  648.3 10.6 fusion.78
  693.0 39.8 %fusion.86 = f32[8,32,48,128]{3,2,1,0:T(8,128)} fusion(f32[8,32,48,128]{3,2,1,0:T(8,128)} %get-tuple-element.306, f32[8,32,47,128]{3,2,1,0:T(8,128)} %get-tuple-element.271, f32[8,32,1,128]{3,2,1,0:T(1,128)} %get-tuple-element.272, f32[8,32,1,128]{3,2,1,0:T(1,128)S(1)} %get-tuple-element.273, f32[8,32,47,128]{3,2,1,0:T(8,128)} %get-tuple-element.274, ...), kind=kLoop, calls=%fused_computation.14.clone.1 | loop fusion | flops 55050240 | bytes 69992464 | tf_op jit(solution)/shard_map/while/body/eval_jaxpr/sub | solution.py:52
  741.7 10.6 fusion.78
  786.4 39.8 %fusion.86 = f32[8,32,48,128]{3,2,1,0:T(8,128)} fusion(f32[8,32,48,128]{3,2,1,0:T(8,128)} %get-tuple-element.306, f32[8,32,47,128]{3,2,1,0:T(8,128)} %get-tuple-element.271, f32[8,32,1,128]{3,2,1,0:T(1,128)} %get-tuple-element.272, f32[8,32,1,128]{3,2,1,0:T(1,128)S(1)} %get-tuple-element.273, f32[8,32,47,128]{3,2,1,0:T(8,128)} %get-tuple-element.274, ...), kind=kLoop, calls=%fused_computation.14.clone.1 | loop fusion | flops 55050240 | bytes 69992464 | tf_op jit(solution)/shard_map/while/body/eval_jaxpr/sub | solution.py:52
  835.0 10.6 fusion.78
  879.8 39.8 %fusion.86 = f32[8,32,48,128]{3,2,1,0:T(8,128)} fusion(f32[8,32,48,128]{3,2,1,0:T(8,128)} %get-tuple-element.306, f32[8,32,47,128]{3,2,1,0:T(8,128)} %get-tuple-element.271, f32[8,32,1,128]{3,2,1,0:T(1,128)} %get-tuple-element.272, f32[8,32,1,128]{3,2,1,0:T(1,128)S(1)} %get-tuple-element.273, f32[8,32,47,128]{3,2,1,0:T(8,128)} %get-tuple-element.274, ...), kind=kLoop, calls=%fused_computation.14.clone.1 | loop fusion | flops 55050240 | bytes 69992464 | tf_op jit(solution)/shard_map/while/body/eval_jaxpr/sub | solution.py:52
  928.4 10.6 fusion.78
  973.1 39.8 %fusion.86 = f32[8,32,48,128]{3,2,1,0:T(8,128)} fusion(f32[8,32,48,128]{3,2,1,0:T(8,128)} %get-tuple-element.306, f32[8,32,47,128]{3,2,1,0:T(8,128)} %get-tuple-element.271, f32[8,32,1,128]{3,2,1,0:T(1,128)} %get-tuple-element.272, f32[8,32,1,128]{3,2,1,0:T(1,128)S(1)} %get-tuple-element.273, f32[8,32,47,128]{3,2,1,0:T(8,128)} %get-tuple-element.274, ...), kind=kLoop, calls=%fused_computation.14.clone.1 | loop fusion | flops 55050240 | bytes 69992464 | tf_op jit(solution)/shard_map/while/body/eval_jaxpr/sub | solution.py:52
  1066.5 39.8 %fusion.86 = f32[8,32,48,128]{3,2,1,0:T(8,128)} fusion(f32[8,32,48,128]{3,2,1,0:T(8,128)} %get-tuple-element.306, f32[8,32,47,128]{3,2,1,0:T(8,128)} %get-tuple-element.271, f32[8,32,1,128]{3,2,1,0:T(1,128)} %get-tuple-element.272, f32[8,32,1,128]{3,2,1,0:T(1,128)S(1)} %get-tuple-element.273, f32[8,32,47,128]{3,2,1,0:T(8,128)} %get-tuple-element.274, ...), kind=kLoop, calls=%fused_computation.14.clone.1 | loop fusion | flops 55050240 | bytes 69992464 | tf_op jit(solution)/shard_map/while/body/eval_jaxpr/sub | solution.py:52
  1115.2 10.6 fusion.78
  1159.9 39.8 %fusion.86 = f32[8,32,48,128]{3,2,1,0:T(8,128)} fusion(f32[8,32,48,128]{3,2,1,0:T(8,128)} %get-tuple-element.306, f32[8,32,47,128]{3,2,1,0:T(8,128)} %get-tuple-element.271, f32[8,32,1,128]{3,2,1,0:T(1,128)} %get-tuple-element.272, f32[8,32,1,128]{3,2,1,0:T(1,128)S(1)} %get-tuple-element.273, f32[8,32,47,128]{3,2,1,0:T(8,128)} %get-tuple-element.274, ...), kind=kLoop, calls=%fused_computation.14.clone.1 | loop fusion | flops 55050240 | bytes 69992464 | tf_op jit(solution)/shard_map/while/body/eval_jaxpr/sub | solution.py:52
  1253.3 39.8 %fusion.86 = f32[8,32,48,128]{3,2,1,0:T(8,128)} fusion(f32[8,32,48,128]{3,2,1,0:T(8,128)} %get-tuple-element.306, f32[8,32,47,128]{3,2,1,0:T(8,128)} %get-tuple-element.271, f32[8,32,1,128]{3,2,1,0:T(1,128)} %get-tuple-element.272, f32[8,32,1,128]{3,2,1,0:T(1,128)S(1)} %get-tuple-element.273, f32[8,32,47,128]{3,2,1,0:T(8,128)} %get-tuple-element.274, ...), kind=kLoop, calls=%fused_computation.14.clone.1 | loop fusion | flops 55050240 | bytes 69992464 | tf_op jit(solution)/shard_map/while/body/eval_jaxpr/sub | solution.py:52
  1302.0 10.6 fusion.78
  1346.7 39.8 %fusion.86 = f32[8,32,48,128]{3,2,1,0:T(8,128)} fusion(f32[8,32,48,128]{3,2,1,0:T(8,128)} %get-tuple-element.306, f32[8,32,47,128]{3,2,1,0:T(8,128)} %get-tuple-element.271, f32[8,32,1,128]{3,2,1,0:T(1,128)} %get-tuple-element.272, f32[8,32,1,128]{3,2,1,0:T(1,128)S(1)} %get-tuple-element.273, f32[8,32,47,128]{3,2,1,0:T(8,128)} %get-tuple-element.274, ...), kind=kLoop, calls=%fused_computation.14.clone.1 | loop fusion | flops 55050240 | bytes 69992464 | tf_op jit(solution)/shard_map/while/body/eval_jaxpr/sub | solution.py:52
  1440.1 39.8 %fusion.86 = f32[8,32,48,128]{3,2,1,0:T(8,128)} fusion(f32[8,32,48,128]{3,2,1,0:T(8,128)} %get-tuple-element.306, f32[8,32,47,128]{3,2,1,0:T(8,128)} %get-tuple-element.271, f32[8,32,1,128]{3,2,1,0:T(1,128)} %get-tuple-element.272, f32[8,32,1,128]{3,2,1,0:T(1,128)S(1)} %get-tuple-element.273, f32[8,32,47,128]{3,2,1,0:T(8,128)} %get-tuple-element.274, ...), kind=kLoop, calls=%fused_computation.14.clone.1 | loop fusion | flops 55050240 | bytes 69992464 | tf_op jit(solution)/shard_map/while/body/eval_jaxpr/sub | solution.py:52
  1506.2 145.7 %all_to_all.19 = f32[8,32,6144]{2,0,1:T(8,128)S(1)} all-to-all(f32[8,32,6144]{2,0,1:T(8,128)S(1)} %bitcast.52), channel_id=1, replica_groups=mesh['cuts'=1,'state'=32] {'state'}, dimensions={1} | all-to-all | bytes 12582912 | tf_op jit(solution)/shard_map/all_to_all | solution.py:73
  1660.5 125.8 %all-reduce.5.cloned.1.call-done = f32[256,256]{0,1:T(8,128)} async-done(((f32[256,256]{0,1:T(8,128)}), f32[256,256]{0,1:T(8,128)}) %all-reduce.5.cloned.1.call-update) | async-done | bytes 262160 | tf_op jit(solution)/shard_map/psum | solution.py:75
  1788.4 11.7 cholesky.50
  1810.5 11.9 cholesky.105
  1828.5 19.7 %custom-call.15 = f32[2,128,128]{1,2,0:T(8,128)S(1)} custom-call(f32[2,128,128]{2,1,0:T(8,128)S(1)} %get-tuple-element.114), custom_call_target="InvertDiagBlocksLowerTriangular" | custom-call | tf_op jit(solution)/shard_map/triangular_solve | solution.py:77
  (322 shorter events, 789.5 us)
Async XLA Ops:
  6.5 1779.8 %all-reduce.5.cloned.1.call-start = ((), (), s32[]{:S(2)}) async-start(), calls=%async_computation.1 | async-start | bytes 524288 | tf_op jit(solution)/shard_map/psum | solution.py:75
  9.2 8.4 copy-start
  88.0 10.6 slice-start
  88.0 10.6 slice-start.1
  181.4 10.6 slice-start
  181.4 10.6 slice-start.1
  274.7 10.6 slice-start
  274.7 10.6 slice-start.1
  368.1 10.6 slice-start
  368.1 10.6 slice-start.1
  461.5 10.6 slice-start
  461.5 10.6 slice-start.1
  554.9 10.6 slice-start
  554.9 10.6 slice-start.1
  648.3 10.6 slice-start
  648.3 10.6 slice-start.1
  741.7 10.6 slice-start
  741.7 10.6 slice-start.1
  835.0 10.6 slice-start
  835.0 10.6 slice-start.1
  928.4 10.6 slice-start
  928.4 10.6 slice-start.1
  1021.8 10.6 slice-start
  1021.8 10.6 slice-start.1
  1115.2 10.6 slice-start
  1115.2 10.6 slice-start.1
  1208.6 10.6 slice-start
  1208.6 10.6 slice-start.1
  1301.9 10.6 slice-start
  1301.9 10.6 slice-start.1
  1395.3 10.6 slice-start
  1395.3 10.6 slice-start.1
  (33 other events, 144.8 us)
Sparse Core Ops, SparseCore 0:
  1660.6 125.6 all-reduce.4
where the time goes:
time: 1880 us; the launch traced here: 1870 us
  local copies, waits for them, and re-layouts  856 us (46%)
  other arithmetic  695 us (37%)
  blocking collectives  146 us (8%)
  waiting for transfers between devices  126 us (7%)
    sub x15, other arithmetic, degree_step(): latest = latest - sigma_now * sigma_next * previous  596 us
    slice x64, local copies, waits for them, and re-layouts, laplace_periodic(): near_sum = jnp.roll(values, 1, axis_dim) + jnp.roll(values, -1, axis_dim)  390 us
    slice x64, local copies, waits for them, and re-layouts, laplace_periodic(): far_sum = jnp.roll(values, 2, axis_dim) + jnp.roll(values, -2, axis_dim)  317 us
    all_to_all x1, blocking collectives, per_device(): lax.all_to_all(flat, 'state', split_axis=1, concat_axis=0, tiled=True)  146 us
    while x150, local copies, waits for them, and re-layouts  133 us
    psum x1, waiting for transfers between devices, per_device(): gram_total = lax.psum(gram_local, 'state')  126 us
  transfers between devices with their start and end apart: 1, of which 1 were waited for; matrix products, arithmetic and copies ran while one was open for 0% of the time, Pallas kernels for 0%

commit v1 on v0

v1 whole, which is shorter than its diff:
```python
import functools
import math

import jax
import jax.numpy as jnp
from jax import lax
from jax.experimental import pallas as pl
from jax.experimental.pallas import tpu as pltpu
from jax.sharding import PartitionSpec as P

DEGREE = 16
ANCHOR_VALUE = -1.125
SUB = 8
LANES = 128
BLOCK = 32
VMEM_LIMIT = 60 * 2**20


def filter_scalars(bounds):
    low_end = bounds[0].astype(jnp.float32) / 64.0
    high_end = bounds[1].astype(jnp.float32) / 16.0
    half_width = (high_end - low_end) / 2.0
    centre = (high_end + low_end) / 2.0
    sigma_now = half_width / (ANCHOR_VALUE - centre)
    tau_value = 2.0 / sigma_now
    scale = sigma_now
    for _ in range(1, DEGREE):
        sigma_now = 1.0 / (tau_value - sigma_now)
        scale = scale * sigma_now
    return jnp.stack(
        [
            (-1.0 / 12.0) / half_width,
            2.0 / half_width,
            3.75 - centre,
            scale,
        ]
    )


def filter_kernel(scal, states, potential, out, weight, first, second):
    depth, rows, lanes = out.shape
    tiles = rows // SUB
    planes = depth
    line_w, twice, shift, scale = (scal[i] for i in range(4))

    @pl.when(pl.program_id(0) == 0)
    def _():
        @pl.loop(0, depth, unroll=8)
        def _(z):
            for t in range(tiles):
                piece = potential[z, pl.ds(t, SUB, stride=tiles), :]
                weight[z, t] = (piece + shift) * twice

        for field in (first, second):
            for edge in (0, 1, depth + 2, depth + 3):
                field[edge] = jnp.zeros(field.shape[1:], jnp.float32)

    @pl.loop(0, depth, unroll=8)
    def _(z):
        out[z] = states[z].astype(jnp.float32)
        for t in range(tiles):
            first[z + 2, t] = out[z, pl.ds(t, SUB, stride=tiles), :]

    wrap = lax.broadcasted_iota(jnp.int32, (lanes, lanes), 0)
    wrap = jnp.abs(wrap - lax.broadcasted_iota(jnp.int32, (lanes, lanes), 1))
    wrap = jnp.minimum(wrap, lanes - wrap)
    ring = jnp.where(wrap == 1, 16.0, jnp.where(wrap == 2, -1.0, 0.0)).astype(jnp.bfloat16)
    ring = jnp.concatenate([ring, ring], axis=0)

    def applied(src, base):
        block = src[pl.ds(base + 2, planes)]
        along = block.reshape(planes * rows, lanes)
        along = dot(jnp.concatenate(split(along), axis=1), ring, ((1,), (0,)))
        along = along.reshape(block.shape)
        for p in range(planes):
            z = base + p
            held = [block[p, t] for t in range(tiles)]
            back = {t: pltpu.roll(held[t], 1, 0) for t in (tiles - 1, tiles - 2)}
            ahead = {t: pltpu.roll(held[t], SUB - 1, 0) for t in (0, 1)}

            def at(t):
                if t < 0:
                    return back[t + tiles]
                if t >= tiles:
                    return ahead[t - tiles]
                return held[t]

            for t in range(tiles):
                near = (at(t - 1) + at(t + 1)) + (src[z + 1, t] + src[z + 3, t])
                far = (at(t - 2) + at(t + 2)) + (src[z, t] + src[z + 4, t])
                total = along[p, t] + (16.0 * near - far)
                yield z, t, total * line_w + held[t] * weight[z, t]

    def step(src, dst):
        @pl.loop(0, depth // planes)
        def _(i):
            for z, t, value in applied(src, i * planes):
                dst[z + 2, t] = value - dst[z + 2, t]

    @pl.loop(0, depth // planes)
    def _(i):
        for z, t, value in applied(first, i * planes):
            second[z + 2, t] = 0.5 * value

    @pl.loop(0, (DEGREE - 2) // 2)
    def _(_):
        step(second, first)
        step(first, second)

    @pl.loop(0, depth // planes)
    def _(i):
        for z, t, value in applied(second, i * planes):
            final = (value - first[z + 2, t]) * scale
            out[z, pl.ds(t, SUB, stride=tiles), :] = final


def run_filter(scal, states, potential, begin, count):
    _, depth, rows, lanes = states.shape
    field = pltpu.VMEM((depth + 4, rows // SUB, SUB, lanes), jnp.float32)
    points = depth * rows * lanes
    return pl.pallas_call(
        filter_kernel,
        grid=(count,),
        in_specs=[
            pl.BlockSpec(memory_space=pltpu.SMEM),
            pl.BlockSpec((None, depth, rows, lanes), lambda i: (begin + i, 0, 0, 0)),
            pl.BlockSpec((depth, rows, lanes), lambda i: (0, 0, 0)),
        ],
        out_specs=pl.BlockSpec((depth, None, rows, lanes), lambda i: (0, i, 0, 0)),
        out_shape=jax.ShapeDtypeStruct((depth, count, rows, lanes), jnp.float32),
        scratch_shapes=[
            pltpu.VMEM((depth, rows // SUB, SUB, lanes), jnp.float32),
            field,
            field,
        ],
        compiler_params=pltpu.CompilerParams(dimension_semantics=("arbitrary",)),
        cost_estimate=pl.CostEstimate(
            flops=18 * DEGREE * points * count,
            bytes_accessed=points * (6 * count + 4),
            transcendentals=0,
        ),
        name=f"filter_{begin}",
    )(scal, states, potential)


def split(value):
    high = value.astype(jnp.bfloat16)
    return high, (value - high.astype(jnp.float32)).astype(jnp.bfloat16)


def dot(left, right, dims):
    return lax.dot_general(left, right, (dims, ((), ())), preferred_element_type=jnp.float32)


def gram_kernel(counts, aligned, *refs):
    pieces, flat, gram, gram_high, gram_cross = refs[:-4], *refs[-4:]
    i = pl.program_id(0)
    first_state = 0
    per_device = sum(counts)
    for piece, count in zip(pieces, counts):
        if aligned:
            sources, _, rows, lanes = piece.shape
            lines = piece.reshape(sources * count * rows, lanes)
        else:
            _, rows, sources, lanes = piece.shape
        for j in range(count):
            for r in range(rows):
                if aligned:
                    value = lines[pl.ds(j * rows + r, sources, stride=count * rows), :]
                else:
                    value = piece[j, r]
                flat[r, pl.ds(first_state + j, sources, stride=per_device), :] = value
        first_state += count
    high, low = split(jnp.concatenate([flat[r] for r in range(flat.shape[0])], axis=1))
    now_high = dot(high, high, ((1,), (1,)))
    now_cross = dot(high, low, ((1,), (1,)))

    @pl.when(i == 0)
    def _():
        gram_high[...] = now_high
        gram_cross[...] = now_cross

    @pl.when(i > 0)
    def _():
        gram_high[...] += now_high
        gram_cross[...] += now_cross

    @pl.when(i == pl.num_programs(0) - 1)
    def _():
        cross = gram_cross[...]
        gram[...] = gram_high[...] + (cross + cross.T)


def run_gram(pieces):
    counts = tuple(p.shape[1] for p in pieces)
    sources, _, rows, lanes = pieces[0].shape
    states = sources * sum(counts)
    tall = SUB if rows % SUB == 0 else rows
    specs = [pl.BlockSpec((sources, c, tall, lanes), lambda i: (0, 0, i, 0)) for c in counts]
    if rows % SUB:
        pieces = [jnp.transpose(p, (1, 2, 0, 3)) for p in pieces]
        specs = [pl.BlockSpec(p.shape, lambda i: (0, 0, 0, 0)) for p in pieces]
    return pl.pallas_call(
        functools.partial(gram_kernel, counts, rows % SUB == 0),
        grid=(rows // tall,),
        in_specs=specs,
        out_specs=[
            pl.BlockSpec((tall, states, lanes), lambda i: (i, 0, 0)),
            pl.BlockSpec((states, states), lambda i: (0, 0)),
        ],
        out_shape=[
            jax.ShapeDtypeStruct((rows, states, lanes), jnp.float32),
            jax.ShapeDtypeStruct((states, states), jnp.float32),
        ],
        scratch_shapes=[pltpu.VMEM((states, states), jnp.float32)] * 2,
        compiler_params=pltpu.CompilerParams(dimension_semantics=("arbitrary",)),
        name="gram",
    )(*pieces)


def exact_dot(left, right, dims):
    return lax.dot_general(
        left,
        right,
        (dims, ((), ())),
        precision=lax.Precision.HIGHEST,
        preferred_element_type=jnp.float32,
    )


def factor_kernel(factor_scale, gram, high, low, work):
    size = gram.shape[0]
    work[:, :size] = gram[...]
    rows = lax.broadcasted_iota(jnp.int32, (size, size), 0)
    cols = lax.broadcasted_iota(jnp.int32, (size, size), 1)
    work[:, size:] = jnp.where(rows == cols, 1.0, 0.0)
    lane = lax.broadcasted_iota(jnp.int32, (BLOCK, LANES), 1)
    line = lax.broadcasted_iota(jnp.int32, (BLOCK, LANES), 0)
    for k in range(0, size, BLOCK):
        diag = work[k : k + BLOCK, k : k + BLOCK]
        unit = jnp.where(lane == line + BLOCK, 1.0, 0.0)
        local = jnp.concatenate([diag, unit[:, BLOCK:]], axis=1)
        pivots = jnp.ones((BLOCK, LANES), jnp.float32)
        for j in range(BLOCK):
            column = jnp.broadcast_to(local[:, j : j + 1], (BLOCK, LANES))
            pivot = column[j : j + 1, :]
            ratio = jnp.where(line > j, column / pivot, 0.0)
            pivots = jnp.where(line == j, jnp.broadcast_to(pivot, pivots.shape), pivots)
            local = local - ratio * local[j : j + 1, :]
        inverse = (local * lax.rsqrt(pivots))[:, BLOCK : 2 * BLOCK]
        panel = exact_dot(inverse, work[k : k + BLOCK, :], ((1,), (0,)))
        work[k : k + BLOCK, :] = panel
        if k + BLOCK < size:
            below = panel[:, k + BLOCK : size]
            work[k + BLOCK :, :] -= exact_dot(below, panel, ((0,), (0,)))
    result = work[:, size:] * factor_scale
    high[...], low[...] = split(result)


def run_factor(gram, factor_scale):
    shape = jax.ShapeDtypeStruct(gram.shape, jnp.bfloat16)
    size = gram.shape[0]
    return pl.pallas_call(
        functools.partial(factor_kernel, factor_scale),
        out_shape=[shape, shape],
        scratch_shapes=[pltpu.VMEM((size, 2 * size), jnp.float32)],
        name="factor",
    )(gram)


def apply_kernel(high, low, flat, out):
    flat_high, flat_low = split(jnp.concatenate([flat[r] for r in range(flat.shape[0])], axis=1))
    total = dot(high[...], flat_low, ((1,), (0,))) + dot(low[...], flat_high, ((1,), (0,)))
    out[...] = dot(high[...], flat_high, ((1,), (0,))) + total


def run_apply(high, low, flat):
    rows, states, lanes = flat.shape
    tall = SUB if rows % SUB == 0 else rows
    whole = pl.BlockSpec((states, states), lambda i: (0, 0))
    return pl.pallas_call(
        apply_kernel,
        grid=(rows // tall,),
        in_specs=[whole, whole, pl.BlockSpec((tall, states, lanes), lambda i: (i, 0, 0))],
        out_specs=pl.BlockSpec((states, tall * lanes), lambda i: (0, i)),
        out_shape=jax.ShapeDtypeStruct((states, rows * lanes), jnp.float32),
        compiler_params=pltpu.CompilerParams(dimension_semantics=("arbitrary",)),
        name="apply",
    )(high, low, flat)


def chunk_counts(states):
    rest = states - 1
    return [c for c in (1, rest // 2, rest - rest // 2) if c]


def per_device(devices, initial_states, potential, bounds):
    states, depth, rows, lanes = initial_states.shape
    points = depth * rows * lanes
    local = points // devices
    scal = filter_scalars(bounds)
    pieces = []
    begin = 0
    for count in chunk_counts(states):
        filtered = run_filter(scal, initial_states, potential, begin, count)
        if devices != depth:
            filtered = jnp.swapaxes(filtered, 0, 1).reshape(count, devices, local // lanes, lanes)
            filtered = jnp.swapaxes(filtered, 0, 1)
        pieces.append(lax.all_to_all(filtered, "state", split_axis=0, concat_axis=0, tiled=True))
        begin += count
    flat, gram = run_gram(pieces)
    total = gram.shape[0]
    blocks = gram.reshape(devices, total // devices, total)
    blocks = lax.all_to_all(blocks, "state", split_axis=0, concat_axis=0, tiled=True)
    mine = jnp.broadcast_to(jnp.sum(blocks, axis=0)[None], blocks.shape)
    gram = lax.all_to_all(mine, "state", split_axis=0, concat_axis=0, tiled=True)
    high, low = run_factor(gram.reshape(total, total), math.sqrt(points))
    return run_apply(high, low, flat)


def solution(mesh):
    return jax.shard_map(
        functools.partial(per_device, mesh.shape["state"]),
        mesh=mesh,
        in_specs=(P(("cuts", "state"), None, None, None), P(), P("cuts")),
        out_specs=P("cuts", "state"),
        check_vma=False,
    )
```

time: 1880 us -> 268 us (0.14)
  local copies, waits for them, and re-layouts: 856 us -> 1.42 us
  other arithmetic: 695 us -> 0.64 us
  Pallas kernels: 0 us -> 128 us
  waiting for transfers between devices: 126 us -> 19.9 us
  blocking collectives: 146 us -> 103 us
    slice x129 -> x1, local copies, waits for them, and re-layouts: 709 us -> 1.39 us  [filter_scalars(): low_end = bounds[0].astype(jnp.float32) / 64.0]
    sub x15 -> x0, other arithmetic: 596 us -> none  [degree_step(): latest = latest - sigma_now * sigma_next * previous]
    while x151 -> x0, local copies, waits for them, and re-layouts: 140 us -> none
    pallas_call x0 -> x6, Pallas kernels: none -> 128 us  [the longest x3 71.3 us: run_filter(): pl.pallas_call(filter_kernel, grid=(count,), in_specs=[pl.BlockSpec(memor...]
    psum x1 -> x0, waiting for transfers between devices: 126 us -> none  [per_device(): gram_total = lax.psum(gram_local, 'state')]
    another operation x9 -> x1, other arithmetic: 53.9 us -> 0.6 us  [filter_scalars(): jnp.stack([-1.0 / 12.0 / half_width, 2.0 / half_width, 3.75 - centre, sca...]
    all_to_all x1 -> x3, blocking collectives: 146 us -> 103 us  [the longest x1 75.4 us: per_device(): lax.all_to_all(filtered, 'state', split_axis=0, concat_axis=0, tiled=True)]
    mul x2 -> x0, other arithmetic: 40.4 us -> none  [the longest x1 37.2 us: filter_states(): (apply_hamiltonian(states, potential) - centre * states) * (sigma_now / h...]
  transfers between devices with their start and end apart: 1 -> 2, of which waited for: 1 -> 1; matrix products, arithmetic and copies ran while one was open for 0% -> 0% of each run, Pallas kernels for 0% -> 23%
where the time goes in v1:
time: 268 us; the launch traced here: 267 us
  Pallas kernels  128 us (48%)
  blocking collectives  103 us (38%)
  waiting for transfers between devices  19.9 us (7%)
  starting transfers between devices  13.2 us (5%)
    all_to_all x1, blocking collectives, per_device(): lax.all_to_all(filtered, 'state', split_axis=0, concat_axis=0, tiled=True)  75.4 us
    pallas_call x3, Pallas kernels, run_filter(): pl.pallas_call(filter_kernel, grid=(count,), in_specs=[pl.BlockSpec(memor...  71.3 us
    pallas_call x1, Pallas kernels, run_factor(): pl.pallas_call(functools.partial(factor_kernel, factor_scale), out_shape=...  38.8 us
    all_to_all x2, waiting for transfers between devices, per_device(): lax.all_to_all(filtered, 'state', split_axis=0, concat_axis=0, tiled=True)  19.9 us
    all_to_all x1, blocking collectives, per_device(): lax.all_to_all(blocks, 'state', split_axis=0, concat_axis=0, tiled=True)  14.2 us
    all_to_all x2, starting transfers between devices, per_device(): lax.all_to_all(filtered, 'state', split_axis=0, concat_axis=0, tiled=True)  13.2 us
    all_to_all x1, blocking collectives, per_device(): lax.all_to_all(mine, 'state', split_axis=0, concat_axis=0, tiled=True)  13 us
    pallas_call x1, Pallas kernels, run_gram(): pl.pallas_call(functools.partial(gram_kernel, counts, rows % SUB == 0), g...  9.31 us
  transfers between devices with their start and end apart: 2, of which 1 were waited for; matrix products, arithmetic and copies ran while one was open for 0% of the time, Pallas kernels for 23%

profile of v1, /device:TPU:0, one launch (start us, length us, event | category | flops | bytes accessed | tf_op | source)
XLA Modules:
  0.0 267.5 jit_solution(17688373566440007747)
XLA Ops:
  0.0 1.4 fusion
  3.5 0.6 pad_maximum_fusion.scal
  4.1 10.3 %filter_0.1 = f32[32,1,48,128]{3,2,1,0:T(8,128)} custom-call(f32[4]{0:T(128)} %pad_maximum_fusion.scal, bf16[8,32,48,128]{3,2,1,0:T(8,128)(2,1)} %states.5, f32[32,48,128]{2,1,0:T(8,128)} %potential.5), custom_call_target="tpu_custom_call" | custom-call | flops 56623104 | bytes 1966080 | tf_op jit(solution)/shard_map/filter_0/pallas_call | solution.py:121
  14.4 7.3 %all-to-all-start = ((f32[32,1,48,128]{3,2,1,0:T(8,128)}), f32[32,1,48,128]{3,2,1,0:T(8,128)S(1)}, u32[]{:S(2)}, u32[]{:S(2)}) async-start(f32[32,1,48,128]{3,2,1,0:T(8,128)} %filter_0.1), calls=%async_computation | async-start | bytes 1572864 | tf_op jit(solution)/shard_map/all_to_all | solution.py:309
  21.7 26.5 %filter_1.1 = f32[32,3,48,128]{3,2,1,0:T(8,128)} custom-call(f32[4]{0:T(128)} %pad_maximum_fusion.scal, bf16[8,32,48,128]{3,2,1,0:T(8,128)(2,1)} %states.5, f32[32,48,128]{2,1,0:T(8,128)} %potential.5), custom_call_target="tpu_custom_call" | custom-call | flops 169869312 | bytes 4325376 | tf_op jit(solution)/shard_map/filter_1/pallas_call | solution.py:121
  48.2 0.0 all-to-all-done.refs_0_
  48.2 0.0 copy-start.1
  48.2 5.8 %all-to-all-start.1 = ((f32[32,3,48,128]{3,2,1,0:T(8,128)}), f32[32,3,48,128]{3,2,1,0:T(8,128)S(1)}, u32[]{:S(2)}, u32[]{:S(2)}) async-start(f32[32,3,48,128]{3,2,1,0:T(8,128)} %filter_1.1), calls=%async_computation.1 | async-start | bytes 4718592 | tf_op jit(solution)/shard_map/all_to_all | solution.py:309
  54.0 34.5 %filter_4.1 = f32[32,4,48,128]{3,2,1,0:T(8,128)} custom-call(f32[4]{0:T(128)} %pad_maximum_fusion.scal, bf16[8,32,48,128]{3,2,1,0:T(8,128)(2,1)} %states.5, f32[32,48,128]{2,1,0:T(8,128)} %potential.5), custom_call_target="tpu_custom_call" | custom-call | flops 226492416 | bytes 5505024 | tf_op jit(solution)/shard_map/filter_4/pallas_call | solution.py:121
  88.6 0.0 copy-done.1
  88.6 19.9 %all-to-all-done.1.refs_1_ = f32[32,3,48,128]{3,2,1,0:T(8,128)S(1)} async-done(((f32[32,3,48,128]{3,2,1,0:T(8,128)}), f32[32,3,48,128]{3,2,1,0:T(8,128)S(1)}, u32[]{:S(2)}, u32[]{:S(2)}) %all-to-all-start.1) | async-done | bytes 2359328 | tf_op jit(solution)/shard_map/all_to_all | solution.py:309
  108.4 0.0 copy-start
  108.4 75.4 %all_to_all.25.refs_2_ = f32[32,4,48,128]{3,2,1,0:T(8,128)} all-to-all(f32[32,4,48,128]{3,2,1,0:T(8,128)} %filter_4.1), channel_id=1, replica_groups=mesh['cuts'=1,'state'=32] {'state'}, dimensions={0} | all-to-all | bytes 6291456 | tf_op jit(solution)/shard_map/all_to_all | solution.py:309
  183.8 0.0 copy-done
  183.8 9.3 %gram.1 = (f32[48,256,128]{2,1,0:T(8,128)}, f32[256,256]{1,0:T(8,128)}) custom-call(f32[32,1,48,128]{3,2,1,0:T(8,128)} %copy-done.1, f32[32,3,48,128]{3,2,1,0:T(8,128)} %copy-done, f32[32,4,48,128]{3,2,1,0:T(8,128)} %all_to_all.25.refs_2_), custom_call_target="tpu_custom_call" | custom-call | tf_op jit(solution)/shard_map/gram/pallas_call | solution.py:203
  193.1 14.2 %all_to_all.26 = f32[32,8,256]{2,1,0:T(8,128)S(1)} all-to-all(f32[32,8,256]{2,1,0:T(8,128)} %bitcast.8), channel_id=1, replica_groups=mesh['cuts'=1,'state'=32] {'state'}, dimensions={0} | all-to-all | bytes 524288 | tf_op jit(solution)/shard_map/all_to_all | solution.py:314
  207.4 13.0 %all_to_all.27 = f32[32,8,256]{2,1,0:T(8,128)} all-to-all(f32[32,8,256]{2,1,0:T(8,128)S(1)} %broadcast_in_dim.2), channel_id=1, replica_groups=mesh['cuts'=1,'state'=32] {'state'}, dimensions={0} | all-to-all | bytes 524288 | tf_op jit(solution)/shard_map/all_to_all | solution.py:316
  220.4 38.8 %factor.1 = (bf16[256,256]{1,0:T(8,128)(2,1)}, bf16[256,256]{1,0:T(8,128)(2,1)}) custom-call(f32[256,256]{1,0:T(8,128)} %bitcast.7), custom_call_target="tpu_custom_call" | custom-call | tf_op jit(solution)/shard_map/factor/pallas_call | solution.py:263
  259.2 8.3 %apply.1 = f32[256,6144]{1,0:T(8,128)} custom-call(bf16[256,256]{1,0:T(8,128)(2,1)} %get-tuple-element.10.high, bf16[256,256]{1,0:T(8,128)(2,1)} %get-tuple-element.11.low, f32[48,256,128]{2,1,0:T(8,128)} %get-tuple-element.12.flat), custom_call_target="tpu_custom_call" | custom-call | tf_op jit(solution)/shard_map/apply/pallas_call | solution.py:281
  (2 shorter events, 0.1 us)
Async XLA Ops:
  14.4 33.8 %all-to-all-start = ((f32[32,1,48,128]{3,2,1,0:T(8,128)}), f32[32,1,48,128]{3,2,1,0:T(8,128)S(1)}, u32[]{:S(2)}, u32[]{:S(2)}) async-start(f32[32,1,48,128]{3,2,1,0:T(8,128)} %filter_0.1), calls=%async_computation | async-start | bytes 1572864 | tf_op jit(solution)/shard_map/all_to_all | solution.py:309
  48.2 40.4 %copy-start.1 = (f32[32,1,48,128]{3,2,1,0:T(8,128)}, f32[32,1,48,128]{3,2,1,0:T(8,128)S(1)}, u32[]{:S(2)}) copy-start(f32[32,1,48,128]{3,2,1,0:T(8,128)S(1)} %all-to-all-done.refs_0_) | copy-start | bytes 2359300
  48.2 60.2 %all-to-all-start.1 = ((f32[32,3,48,128]{3,2,1,0:T(8,128)}), f32[32,3,48,128]{3,2,1,0:T(8,128)S(1)}, u32[]{:S(2)}, u32[]{:S(2)}) async-start(f32[32,3,48,128]{3,2,1,0:T(8,128)} %filter_1.1), calls=%async_computation.1 | async-start | bytes 4718592 | tf_op jit(solution)/shard_map/all_to_all | solution.py:309
  108.4 75.4 %copy-start = (f32[32,3,48,128]{3,2,1,0:T(8,128)}, f32[32,3,48,128]{3,2,1,0:T(8,128)S(1)}, u32[]{:S(2)}) copy-start(f32[32,3,48,128]{3,2,1,0:T(8,128)S(1)} %all-to-all-done.1.refs_1_) | copy-start | bytes 7077892

commit v2 on v1

--- a/solution.py
+++ b/solution.py
@@ -228,6 +228,44 @@
     )
 
 
+def eliminate(tiles):
+    count = len(tiles)
+    shape = tiles[0].shape
+    line = lax.broadcasted_iota(jnp.int32, shape, 0)
+
+    def row(tile, c):
+        return jnp.broadcast_to(tile[c : c + 1, :], shape)
+
+    cols = [
+        {g: jnp.broadcast_to(tiles[g][:, d : d + 1], shape) for g in range(d // SUB, count)}
+        for d in range(count * SUB)
+    ]
+    scales = [jnp.ones(shape, jnp.float32) for _ in range(count)]
+    for j in range(0, count * SUB, 2):
+        own, c = j // SUB, j % SUB
+        left, right = cols[j], cols[j + 1]
+        p, q, s = row(left[own], c), row(left[own], c + 1), row(right[own], c + 1)
+        inverse = 1.0 / (p * s - q * q)
+        p_in, q_in, s_in = p * inverse, q * inverse, s * inverse
+        ratio = q / p
+        row_left, row_right = row(tiles[own], c), row(tiles[own], c + 1)
+        scales[own] = jnp.where(line == c, p, scales[own])
+        scales[own] = jnp.where(line == c + 1, s - q * ratio, scales[own])
+        first, second = {}, {}
+        for g in range(own, count):
+            first[g] = left[g] * s_in - right[g] * q_in
+            second[g] = right[g] * p_in - left[g] * q_in
+        first[own] = jnp.where(line > c + 1, first[own], jnp.where(line == c + 1, ratio, 0.0))
+        second[own] = jnp.where(line > c + 1, second[own], 0.0)
+        for d in range(j + 2, count * SUB):
+            x, y = row(left[d // SUB], d % SUB), row(right[d // SUB], d % SUB)
+            for g in range(d // SUB, count):
+                cols[d][g] = cols[d][g] - (first[g] * x + second[g] * y)
+        for g in range(own, count):
+            tiles[g] = tiles[g] - (first[g] * row_left + second[g] * row_right)
+    return [t * lax.rsqrt(v) for t, v in zip(tiles, scales)]
+
+
 def factor_kernel(factor_scale, gram, high, low, work):
     size = gram.shape[0]
     work[:, :size] = gram[...]
@@ -236,18 +274,12 @@
     work[:, size:] = jnp.where(rows == cols, 1.0, 0.0)
     lane = lax.broadcasted_iota(jnp.int32, (BLOCK, LANES), 1)
     line = lax.broadcasted_iota(jnp.int32, (BLOCK, LANES), 0)
+    unit = jnp.where(lane == line + BLOCK, 1.0, 0.0)
     for k in range(0, size, BLOCK):
         diag = work[k : k + BLOCK, k : k + BLOCK]
-        unit = jnp.where(lane == line + BLOCK, 1.0, 0.0)
         local = jnp.concatenate([diag, unit[:, BLOCK:]], axis=1)
-        pivots = jnp.ones((BLOCK, LANES), jnp.float32)
-        for j in range(BLOCK):
-            column = jnp.broadcast_to(local[:, j : j + 1], (BLOCK, LANES))
-            pivot = column[j : j + 1, :]
-            ratio = jnp.where(line > j, column / pivot, 0.0)
-            pivots = jnp.where(line == j, jnp.broadcast_to(pivot, pivots.shape), pivots)
-            local = local - ratio * local[j : j + 1, :]
-        inverse = (local * lax.rsqrt(pivots))[:, BLOCK : 2 * BLOCK]
+        tiles = eliminate([local[i : i + SUB] for i in range(0, BLOCK, SUB)])
+        inverse = jnp.concatenate(tiles, axis=0)[:, BLOCK : 2 * BLOCK]
         panel = exact_dot(inverse, work[k : k + BLOCK, :], ((1,), (0,)))
         work[k : k + BLOCK, :] = panel
         if k + BLOCK < size:

time: 268 us -> 242 us (0.903)
  Pallas kernels: 128 us -> 101 us
    pallas_call x1, Pallas kernels: 38.8 us -> 12.4 us  [run_factor(): pl.pallas_call(functools.partial(factor_kernel, factor_scale), out_shape=...]
  transfers between devices with their start and end apart: 2 -> 2, of which waited for: 1 -> 1; matrix products, arithmetic and copies ran while one was open for 0% -> 0% of each run, Pallas kernels for 23% -> 25%
where the time goes in v2:
time: 242 us; the launch traced here: 241 us
  blocking collectives  103 us (43%)
  Pallas kernels  101 us (42%)
  waiting for transfers between devices  19.9 us (8%)
  starting transfers between devices  13.2 us (5%)
    all_to_all x1, blocking collectives, per_device(): lax.all_to_all(filtered, 'state', split_axis=0, concat_axis=0, tiled=True)  75.4 us
    pallas_call x3, Pallas kernels, run_filter(): pl.pallas_call(filter_kernel, grid=(count,), in_specs=[pl.BlockSpec(memor...  71.3 us
    all_to_all x2, waiting for transfers between devices, per_device(): lax.all_to_all(filtered, 'state', split_axis=0, concat_axis=0, tiled=True)  19.9 us
    all_to_all x1, blocking collectives, per_device(): lax.all_to_all(blocks, 'state', split_axis=0, concat_axis=0, tiled=True)  14.2 us
    all_to_all x2, starting transfers between devices, per_device(): lax.all_to_all(filtered, 'state', split_axis=0, concat_axis=0, tiled=True)  13.2 us
    all_to_all x1, blocking collectives, per_device(): lax.all_to_all(mine, 'state', split_axis=0, concat_axis=0, tiled=True)  13 us
    pallas_call x1, Pallas kernels, run_factor(): pl.pallas_call(functools.partial(factor_kernel, factor_scale), out_shape=...  12.4 us
    pallas_call x1, Pallas kernels, run_gram(): pl.pallas_call(functools.partial(gram_kernel, counts, rows % SUB == 0), g...  9.31 us
  transfers between devices with their start and end apart: 2, of which 1 were waited for; matrix products, arithmetic and copies ran while one was open for 0% of the time, Pallas kernels for 25%

profile of v2, /device:TPU:0, one launch (start us, length us, event | category | flops | bytes accessed | tf_op | source)
XLA Modules:
  0.0 241.1 jit_solution(496227103913637634)
XLA Ops:
  0.0 1.4 fusion
  3.5 0.6 pad_maximum_fusion.scal
  4.1 10.3 %filter_0.1 = f32[32,1,48,128]{3,2,1,0:T(8,128)} custom-call(f32[4]{0:T(128)} %pad_maximum_fusion.scal, bf16[8,32,48,128]{3,2,1,0:T(8,128)(2,1)} %states.5, f32[32,48,128]{2,1,0:T(8,128)} %potential.5), custom_call_target="tpu_custom_call" | custom-call | flops 56623104 | bytes 1966080 | tf_op jit(solution)/shard_map/filter_0/pallas_call | solution.py:121
  14.4 7.3 %all-to-all-start = ((f32[32,1,48,128]{3,2,1,0:T(8,128)}), f32[32,1,48,128]{3,2,1,0:T(8,128)S(1)}, u32[]{:S(2)}, u32[]{:S(2)}) async-start(f32[32,1,48,128]{3,2,1,0:T(8,128)} %filter_0.1), calls=%async_computation | async-start | bytes 1572864 | tf_op jit(solution)/shard_map/all_to_all | solution.py:341
  21.7 26.5 %filter_1.1 = f32[32,3,48,128]{3,2,1,0:T(8,128)} custom-call(f32[4]{0:T(128)} %pad_maximum_fusion.scal, bf16[8,32,48,128]{3,2,1,0:T(8,128)(2,1)} %states.5, f32[32,48,128]{2,1,0:T(8,128)} %potential.5), custom_call_target="tpu_custom_call" | custom-call | flops 169869312 | bytes 4325376 | tf_op jit(solution)/shard_map/filter_1/pallas_call | solution.py:121
  48.2 0.0 all-to-all-done.refs_0_
  48.2 0.0 copy-start.1
  48.2 5.8 %all-to-all-start.1 = ((f32[32,3,48,128]{3,2,1,0:T(8,128)}), f32[32,3,48,128]{3,2,1,0:T(8,128)S(1)}, u32[]{:S(2)}, u32[]{:S(2)}) async-start(f32[32,3,48,128]{3,2,1,0:T(8,128)} %filter_1.1), calls=%async_computation.1 | async-start | bytes 4718592 | tf_op jit(solution)/shard_map/all_to_all | solution.py:341
  54.0 34.5 %filter_4.1 = f32[32,4,48,128]{3,2,1,0:T(8,128)} custom-call(f32[4]{0:T(128)} %pad_maximum_fusion.scal, bf16[8,32,48,128]{3,2,1,0:T(8,128)(2,1)} %states.5, f32[32,48,128]{2,1,0:T(8,128)} %potential.5), custom_call_target="tpu_custom_call" | custom-call | flops 226492416 | bytes 5505024 | tf_op jit(solution)/shard_map/filter_4/pallas_call | solution.py:121
  88.6 0.0 copy-done.1
  88.6 19.9 %all-to-all-done.1.refs_1_ = f32[32,3,48,128]{3,2,1,0:T(8,128)S(1)} async-done(((f32[32,3,48,128]{3,2,1,0:T(8,128)}), f32[32,3,48,128]{3,2,1,0:T(8,128)S(1)}, u32[]{:S(2)}, u32[]{:S(2)}) %all-to-all-start.1) | async-done | bytes 2359328 | tf_op jit(solution)/shard_map/all_to_all | solution.py:341
  108.4 0.0 copy-start
  108.4 75.4 %all_to_all.25.refs_2_ = f32[32,4,48,128]{3,2,1,0:T(8,128)} all-to-all(f32[32,4,48,128]{3,2,1,0:T(8,128)} %filter_4.1), channel_id=1, replica_groups=mesh['cuts'=1,'state'=32] {'state'}, dimensions={0} | all-to-all | bytes 6291456 | tf_op jit(solution)/shard_map/all_to_all | solution.py:341
  183.8 0.0 copy-done
  183.8 9.3 %gram.1 = (f32[48,256,128]{2,1,0:T(8,128)}, f32[256,256]{1,0:T(8,128)}) custom-call(f32[32,1,48,128]{3,2,1,0:T(8,128)} %copy-done.1, f32[32,3,48,128]{3,2,1,0:T(8,128)} %copy-done, f32[32,4,48,128]{3,2,1,0:T(8,128)} %all_to_all.25.refs_2_), custom_call_target="tpu_custom_call" | custom-call | tf_op jit(solution)/shard_map/gram/pallas_call | solution.py:203
  193.1 14.2 %all_to_all.26 = f32[32,8,256]{2,1,0:T(8,128)S(1)} all-to-all(f32[32,8,256]{2,1,0:T(8,128)} %bitcast.8), channel_id=1, replica_groups=mesh['cuts'=1,'state'=32] {'state'}, dimensions={0} | all-to-all | bytes 524288 | tf_op jit(solution)/shard_map/all_to_all | solution.py:346
  207.4 13.0 %all_to_all.27 = f32[32,8,256]{2,1,0:T(8,128)} all-to-all(f32[32,8,256]{2,1,0:T(8,128)S(1)} %broadcast_in_dim.2), channel_id=1, replica_groups=mesh['cuts'=1,'state'=32] {'state'}, dimensions={0} | all-to-all | bytes 524288 | tf_op jit(solution)/shard_map/all_to_all | solution.py:348
  220.4 12.4 %factor.1 = (bf16[256,256]{1,0:T(8,128)(2,1)}, bf16[256,256]{1,0:T(8,128)(2,1)}) custom-call(f32[256,256]{1,0:T(8,128)} %bitcast.7), custom_call_target="tpu_custom_call" | custom-call | tf_op jit(solution)/shard_map/factor/pallas_call | solution.py:295
  232.8 8.3 %apply.1 = f32[256,6144]{1,0:T(8,128)} custom-call(bf16[256,256]{1,0:T(8,128)(2,1)} %get-tuple-element.10.high, bf16[256,256]{1,0:T(8,128)(2,1)} %get-tuple-element.11.low, f32[48,256,128]{2,1,0:T(8,128)} %get-tuple-element.12.flat), custom_call_target="tpu_custom_call" | custom-call | tf_op jit(solution)/shard_map/apply/pallas_call | solution.py:313
  (2 shorter events, 0.1 us)
Async XLA Ops:
  14.4 33.8 %all-to-all-start = ((f32[32,1,48,128]{3,2,1,0:T(8,128)}), f32[32,1,48,128]{3,2,1,0:T(8,128)S(1)}, u32[]{:S(2)}, u32[]{:S(2)}) async-start(f32[32,1,48,128]{3,2,1,0:T(8,128)} %filter_0.1), calls=%async_computation | async-start | bytes 1572864 | tf_op jit(solution)/shard_map/all_to_all | solution.py:341
  48.2 40.4 %copy-start.1 = (f32[32,1,48,128]{3,2,1,0:T(8,128)}, f32[32,1,48,128]{3,2,1,0:T(8,128)S(1)}, u32[]{:S(2)}) copy-start(f32[32,1,48,128]{3,2,1,0:T(8,128)S(1)} %all-to-all-done.refs_0_) | copy-start | bytes 2359300
  48.2 60.2 %all-to-all-start.1 = ((f32[32,3,48,128]{3,2,1,0:T(8,128)}), f32[32,3,48,128]{3,2,1,0:T(8,128)S(1)}, u32[]{:S(2)}, u32[]{:S(2)}) async-start(f32[32,3,48,128]{3,2,1,0:T(8,128)} %filter_1.1), calls=%async_computation.1 | async-start | bytes 4718592 | tf_op jit(solution)/shard_map/all_to_all | solution.py:341
  108.4 75.4 %copy-start = (f32[32,3,48,128]{3,2,1,0:T(8,128)}, f32[32,3,48,128]{3,2,1,0:T(8,128)S(1)}, u32[]{:S(2)}) copy-start(f32[32,3,48,128]{3,2,1,0:T(8,128)S(1)} %all-to-all-done.1.refs_1_) | copy-start | bytes 7077892

commit v3 on v2

v3 whole, which is shorter than its diff:
```python
import functools
import math

import jax
import jax.numpy as jnp
from jax import lax
from jax.experimental import pallas as pl
from jax.experimental.pallas import tpu as pltpu
from jax.sharding import PartitionSpec as P

DEGREE = 16
ANCHOR_VALUE = -1.125
SUB = 8
LANES = 128
BLOCK = 32


def filter_scalars(bounds, shape):
    low_end = jnp.full(shape, bounds[0], jnp.int32).astype(jnp.float32) / 64.0
    high_end = jnp.full(shape, bounds[1], jnp.int32).astype(jnp.float32) / 16.0
    half_width = (high_end - low_end) / 2.0
    centre = (high_end + low_end) / 2.0
    sigma_now = half_width / (ANCHOR_VALUE - centre)
    tau_value = 2.0 / sigma_now
    scale = sigma_now
    for _ in range(1, DEGREE):
        sigma_now = 1.0 / (tau_value - sigma_now)
        scale = scale * sigma_now
    return (-1.0 / 12.0) / half_width, 2.0 / half_width, 3.75 - centre, scale


def filter_kernel(bounds, states, potential, out, weight, first, second):
    depth, rows, lanes = out.shape
    tiles = rows // SUB
    line_w, twice, shift, scale = filter_scalars(bounds, (SUB, lanes))

    @pl.when(pl.program_id(0) == 0)
    def _():
        @pl.loop(0, depth, unroll=8)
        def _(z):
            for t in range(tiles):
                piece = potential[z, pl.ds(t, SUB, stride=tiles), :]
                weight[z, t] = (piece + shift) * twice

        for field in (first, second):
            for edge in (0, 1, depth + 2, depth + 3):
                field[edge] = jnp.zeros(field.shape[1:], jnp.float32)

    @pl.loop(0, depth, unroll=8)
    def _(z):
        out[z] = states[z].astype(jnp.float32)
        for t in range(tiles):
            first[z + 2, t] = out[z, pl.ds(t, SUB, stride=tiles), :]

    wrap = lax.broadcasted_iota(jnp.int32, (lanes, lanes), 0)
    wrap = jnp.abs(wrap - lax.broadcasted_iota(jnp.int32, (lanes, lanes), 1))
    wrap = jnp.minimum(wrap, lanes - wrap)
    ring = jnp.where(wrap == 1, 16.0, jnp.where(wrap == 2, -1.0, 0.0)).astype(jnp.bfloat16)
    ring = jnp.concatenate([ring, ring], axis=0)

    def applied(src):
        block = src[2 : depth + 2]
        along = block.reshape(depth * rows, lanes)
        along = dot(jnp.concatenate(split(along), axis=1), ring, ((1,), (0,)))
        along = along.reshape(block.shape)
        for z in range(depth):
            held = [block[z, t] for t in range(tiles)]
            back = {t: pltpu.roll(held[t], 1, 0) for t in (tiles - 1, tiles - 2)}
            ahead = {t: pltpu.roll(held[t], SUB - 1, 0) for t in (0, 1)}

            def at(t):
                if t < 0:
                    return back[t + tiles]
                if t >= tiles:
                    return ahead[t - tiles]
                return held[t]

            for t in range(tiles):
                near = (at(t - 1) + at(t + 1)) + (src[z + 1, t] + src[z + 3, t])
                far = (at(t - 2) + at(t + 2)) + (src[z, t] + src[z + 4, t])
                total = along[z, t] + (16.0 * near - far)
                yield z, t, total * line_w + held[t] * weight[z, t]

    def step(src, dst):
        for z, t, value in applied(src):
            dst[z + 2, t] = value - dst[z + 2, t]

    for z, t, value in applied(first):
        second[z + 2, t] = 0.5 * value

    @pl.loop(0, (DEGREE - 2) // 2)
    def _(_):
        step(second, first)
        step(first, second)

    for z, t, value in applied(second):
        out[z, pl.ds(t, SUB, stride=tiles), :] = (value - first[z + 2, t]) * scale


def run_filter(bounds, states, potential, begin, count):
    _, depth, rows, lanes = states.shape
    points = depth * rows * lanes
    field = pltpu.VMEM((depth + 4, rows // SUB, SUB, lanes), jnp.float32)
    return pl.pallas_call(
        filter_kernel,
        grid=(count,),
        in_specs=[
            pl.BlockSpec(memory_space=pltpu.SMEM),
            pl.BlockSpec((None, depth, rows, lanes), lambda i: (begin + i, 0, 0, 0)),
            pl.BlockSpec((depth, rows, lanes), lambda i: (0, 0, 0)),
        ],
        out_specs=pl.BlockSpec((depth, None, rows, lanes), lambda i: (0, i, 0, 0)),
        out_shape=jax.ShapeDtypeStruct((depth, count, rows, lanes), jnp.float32),
        scratch_shapes=[
            pltpu.VMEM((depth, rows // SUB, SUB, lanes), jnp.float32),
            field,
            field,
        ],
        compiler_params=pltpu.CompilerParams(dimension_semantics=("arbitrary",)),
        cost_estimate=pl.CostEstimate(
            flops=18 * DEGREE * points * count,
            bytes_accessed=points * (6 * count + 4),
            transcendentals=0,
        ),
        name=f"filter_{begin}",
    )(bounds, states, potential)


def split(value):
    high = value.astype(jnp.bfloat16)
    return high, (value - high.astype(jnp.float32)).astype(jnp.bfloat16)


def dot(left, right, dims):
    return lax.dot_general(left, right, (dims, ((), ())), preferred_element_type=jnp.float32)


def gather(pieces, tall, high, low):
    i = pl.program_id(0)
    begin = 0
    for piece in pieces:
        sources, count, _, lanes = piece.shape
        for j in range(count):
            where = slice(begin + j * sources, begin + (j + 1) * sources)
            value = jnp.swapaxes(piece[:, j, pl.ds(i * tall, tall), :], 0, 1)
            for r in range(tall):
                columns = slice(r * lanes, (r + 1) * lanes)
                high[where, columns], low[where, columns] = split(value[r])
        begin += count * sources


def accumulate(pairs):
    @pl.when(pl.program_id(0) == 0)
    def _():
        for ref, value in pairs:
            ref[...] = value

    @pl.when(pl.program_id(0) > 0)
    def _():
        for ref, value in pairs:
            ref[...] += value


def early_kernel(tall, *refs):
    *pieces, high, low, gram, same, cross = refs
    gather(pieces, tall, high, low)
    left = high[...]
    accumulate(
        [
            (same, dot(left, left, ((1,), (1,)))),
            (cross, dot(left, low[...], ((1,), (1,)))),
        ]
    )

    @pl.when(pl.program_id(0) == pl.num_programs(0) - 1)
    def _():
        gram[...] = same[...] + (cross[...] + cross[...].T)


def late_kernel(tall, early_high, early_low, early_gram, piece, *refs):
    high, low, gram, same, cross = refs
    gather([piece], tall, high, low)
    sources = piece.shape[0]
    old = early_high.shape[0]
    new = high.shape[0]
    left = high[...]
    both = jnp.concatenate([left, low[...]], axis=0)
    kept = jnp.concatenate([early_high[...], left], axis=0)
    accumulate(
        [
            (same, dot(both, kept, ((1,), (1,)))),
            (cross, dot(left, early_low[...], ((1,), (1,)))),
        ]
    )

    @pl.when(pl.program_id(0) == pl.num_programs(0) - 1)
    def _():
        total = old + new
        mixed = same[:new, :old] + (same[new:, :old] + cross[...])
        tail = same[new:, old:]
        own = same[:new, old:] + (tail + tail.T)
        top = jnp.concatenate([early_gram[...], mixed.T], axis=1)
        whole = jnp.concatenate([top, jnp.concatenate([mixed, own], axis=1)], axis=0)
        lines = gram.reshape(gram.shape[0] * gram.shape[1], LANES)
        per_device = total // sources
        for half in range(total // LANES):
            for c in range(per_device):
                where = pl.ds(half * per_device + c, sources, stride=gram.shape[1])
                block = whole[c * sources : (c + 1) * sources, half * LANES : (half + 1) * LANES]
                lines[where, :] = block


def run_gram(pieces):
    sources, _, rows, lanes = pieces[0].shape
    counts = [p.shape[1] for p in pieces]
    new = sources * counts[-1]
    old = sources * sum(counts[:-1])
    total = old + new
    tall = SUB if rows % SUB == 0 else rows
    points = rows * lanes
    resident = pl.BlockSpec(memory_space=pltpu.VMEM)

    def columns(count):
        return pl.BlockSpec((count, tall * lanes), lambda i: (0, i))

    def pair(count):
        return [jax.ShapeDtypeStruct((count, points), jnp.bfloat16)] * 2

    def fixed(*shape):
        return pl.BlockSpec(shape, lambda i: (0,) * len(shape))

    params = pltpu.CompilerParams(dimension_semantics=("arbitrary",))
    early_high, early_low, early_gram = pl.pallas_call(
        functools.partial(early_kernel, tall),
        grid=(rows // tall,),
        in_specs=[resident] * (len(pieces) - 1),
        out_specs=[columns(old), columns(old), fixed(old, old)],
        out_shape=[*pair(old), jax.ShapeDtypeStruct((old, old), jnp.float32)],
        scratch_shapes=[pltpu.VMEM((old, old), jnp.float32)] * 2,
        compiler_params=params,
        cost_estimate=pl.CostEstimate(
            flops=4 * old * old * points, bytes_accessed=8 * old * points, transcendentals=0
        ),
        name="early_gram",
    )(*pieces[:-1])
    blocks = (sources, total // LANES * (total // sources), LANES)
    high, low, gram = pl.pallas_call(
        functools.partial(late_kernel, tall),
        grid=(rows // tall,),
        in_specs=[columns(old), columns(old), fixed(old, old), resident],
        out_specs=[columns(new), columns(new), fixed(*blocks)],
        out_shape=[*pair(new), jax.ShapeDtypeStruct(blocks, jnp.float32)],
        scratch_shapes=[
            pltpu.VMEM((2 * new, total), jnp.float32),
            pltpu.VMEM((new, old), jnp.float32),
        ],
        compiler_params=params,
        name="late_gram",
    )(early_high, early_low, early_gram, pieces[-1])
    return (early_high, early_low, high, low), gram


def exact_dot(left, right, dims):
    return lax.dot_general(
        left,
        right,
        (dims, ((), ())),
        precision=lax.Precision.HIGHEST,
        preferred_element_type=jnp.float32,
    )


def eliminate(tiles):
    count = len(tiles)
    shape = tiles[0].shape
    line = lax.broadcasted_iota(jnp.int32, shape, 0)

    def row(tile, c):
        return jnp.broadcast_to(tile[c : c + 1, :], shape)

    cols = [
        {g: jnp.broadcast_to(tiles[g][:, d : d + 1], shape) for g in range(d // SUB, count)}
        for d in range(count * SUB)
    ]
    scales = [jnp.ones(shape, jnp.float32) for _ in range(count)]
    for j in range(0, count * SUB, 2):
        own, c = j // SUB, j % SUB
        left, right = cols[j], cols[j + 1]
        p, q, s = row(left[own], c), row(left[own], c + 1), row(right[own], c + 1)
        inverse = 1.0 / (p * s - q * q)
        p_in, q_in, s_in = p * inverse, q * inverse, s * inverse
        ratio = q / p
        row_left, row_right = row(tiles[own], c), row(tiles[own], c + 1)
        scales[own] = jnp.where(line == c, p, scales[own])
        scales[own] = jnp.where(line == c + 1, s - q * ratio, scales[own])
        first, second = {}, {}
        for g in range(own, count):
            first[g] = left[g] * s_in - right[g] * q_in
            second[g] = right[g] * p_in - left[g] * q_in
        first[own] = jnp.where(line > c + 1, first[own], jnp.where(line == c + 1, ratio, 0.0))
        second[own] = jnp.where(line > c + 1, second[own], 0.0)
        for d in range(j + 2, count * SUB):
            x, y = row(left[d // SUB], d % SUB), row(right[d // SUB], d % SUB)
            for g in range(d // SUB, count):
                cols[d][g] = cols[d][g] - (first[g] * x + second[g] * y)
        for g in range(own, count):
            tiles[g] = tiles[g] - (first[g] * row_left + second[g] * row_right)
    return [t * lax.rsqrt(v) for t, v in zip(tiles, scales)]


def finish_kernel(factor_scale, gram, *refs):
    rows, out, work, turn, right, stage, arrive, leave = refs[:4], *refs[4:]
    begin = (0, rows[0].shape[0])
    copies = [
        pltpu.make_async_copy(
            ref, right.at[i % 2, pl.ds(begin[i // 2], ref.shape[0])], arrive.at[i]
        )
        for i, ref in enumerate(rows)
    ]
    for copy in copies:
        copy.start()
    high, low = invert_factor(factor_scale, gram, work, turn)
    both = jnp.concatenate([high, low], axis=0)
    for copy in copies:
        copy.wait()
    size, wide = stage.shape[1:]
    sent = []
    for t in range(out.shape[1] // wide):
        columns = pl.ds(t * wide, wide)
        main = dot(both, right[0, :, columns], ((1,), (0,)))
        rest = dot(high, right[1, :, columns], ((1,), (0,)))
        if t >= 2:
            sent[t - 2].wait()
        stage[t % 2] = main[:size] + (main[size:] + rest)
        sent.append(pltpu.make_async_copy(stage.at[t % 2], out.at[:, columns], leave.at[t % 2]))
        sent[t].start()
    for copy in sent[-2:]:
        copy.wait()


def invert_factor(factor_scale, gram, work, turn):
    size = work.shape[0]
    sources, stride, _ = gram.shape
    halves = size // LANES
    per_device = size // sources
    lines = gram.reshape(sources * stride, LANES)
    for half in range(halves):
        for c in range(per_device):
            block = lines[pl.ds(half * per_device + c, sources, stride=stride), :]
            turn[half, pl.ds(c, sources, stride=per_device), :] = block
    whole = jnp.concatenate([turn[k] for k in range(halves)], axis=1).T
    to_states(whole, sources, turn)
    for k in range(halves):
        work[:, k * LANES : (k + 1) * LANES] = turn[k]
    rows = lax.broadcasted_iota(jnp.int32, (size, size), 0)
    cols = lax.broadcasted_iota(jnp.int32, (size, size), 1)
    work[:, size:] = jnp.where(rows == cols, 1.0, 0.0)
    lane = lax.broadcasted_iota(jnp.int32, (BLOCK, LANES), 1)
    line = lax.broadcasted_iota(jnp.int32, (BLOCK, LANES), 0)
    unit = jnp.where(lane == line + BLOCK, 1.0, 0.0)
    for k in range(0, size, BLOCK):
        diag = work[k : k + BLOCK, k : k + BLOCK]
        local = jnp.concatenate([diag, unit[:, BLOCK:]], axis=1)
        tiles = eliminate([local[i : i + SUB] for i in range(0, BLOCK, SUB)])
        inverse = jnp.concatenate(tiles, axis=0)[:, BLOCK : 2 * BLOCK]
        panel = exact_dot(inverse, work[k : k + BLOCK, :], ((1,), (0,)))
        work[k : k + BLOCK, :] = panel
        if k + BLOCK < size:
            below = panel[:, k + BLOCK : size]
            work[k + BLOCK :, :] -= exact_dot(below, panel, ((0,), (0,)))
    mixed = (work[:, size:] * factor_scale).T
    for k in range(halves):
        turn[k] = mixed[:, k * LANES : (k + 1) * LANES]
    columns = [
        jnp.concatenate(
            [turn[k, pl.ds(c, sources, stride=per_device), :] for c in range(per_device)], axis=0
        )
        for k in range(halves)
    ]
    return split(jnp.concatenate(columns, axis=1).T)


def to_states(whole, sources, turn):
    size = whole.shape[0]
    per_device = size // sources
    for c in range(per_device):
        for k in range(size // LANES):
            block = whole[c * sources : (c + 1) * sources, k * LANES : (k + 1) * LANES]
            turn[k, pl.ds(c, sources, stride=per_device), :] = block


def run_finish(gram, rows, factor_scale):
    sources, stride, lanes = gram.shape
    size = math.isqrt(sources * stride * lanes)
    points = rows[0].shape[1]
    wide = 1024 if points % 1024 == 0 else 512
    anywhere = pl.BlockSpec(memory_space=pl.ANY)
    return pl.pallas_call(
        functools.partial(finish_kernel, factor_scale),
        in_specs=[pl.BlockSpec(memory_space=pltpu.VMEM)] + [anywhere] * len(rows),
        out_specs=anywhere,
        out_shape=jax.ShapeDtypeStruct((size, points), jnp.float32),
        scratch_shapes=[
            pltpu.VMEM((size, 2 * size), jnp.float32),
            pltpu.VMEM((size // LANES, size, LANES), jnp.float32),
            pltpu.VMEM((2, size, points), jnp.bfloat16),
            pltpu.VMEM((2, size, wide), jnp.float32),
            pltpu.SemaphoreType.DMA((len(rows),)),
            pltpu.SemaphoreType.DMA((2,)),
        ],
        name="finish",
    )(gram, *rows)


def chunk_counts(states):
    edge = max(states // 4, 1)
    return [c for c in (edge, states - 2 * edge, edge) if c > 0]


def per_device(devices, initial_states, potential, bounds):
    states, depth, rows, lanes = initial_states.shape
    points = depth * rows * lanes
    local = points // devices
    pieces = []
    begin = 0
    for count in chunk_counts(states):
        filtered = run_filter(bounds, initial_states, potential, begin, count)
        if devices != depth:
            filtered = jnp.swapaxes(filtered, 0, 1).reshape(count, devices, local // lanes, lanes)
            filtered = jnp.swapaxes(filtered, 0, 1)
        pieces.append(lax.all_to_all(filtered, "state", split_axis=0, concat_axis=0, tiled=True))
        begin += count
    rows, gram = run_gram(pieces)
    gram = lax.all_to_all(gram, "state", split_axis=0, concat_axis=0, tiled=True)
    gram = jnp.broadcast_to(jnp.sum(gram, axis=0)[None], gram.shape)
    gram = lax.all_to_all(gram, "state", split_axis=0, concat_axis=0, tiled=True)
    return run_finish(gram, rows, math.sqrt(points))


def solution(mesh):
    return jax.shard_map(
        functools.partial(per_device, mesh.shape["state"]),
        mesh=mesh,
        in_specs=(P(("cuts", "state"), None, None, None), P(), P("cuts")),
        out_specs=P("cuts", "state"),
        check_vma=False,
    )
```

time: 242 us -> 237 us (0.979)
  blocking collectives: 103 us -> 27.4 us
  waiting for transfers between devices: 19.9 us -> 83 us
  Pallas kernels: 101 us -> 109 us
  starting transfers between devices: 13.2 us -> 15.8 us
    all_to_all x3 -> x2, blocking collectives: 103 us -> 27.4 us  [per_device(): lax.all_to_all(gram, 'state', split_axis=0, concat_axis=0, tiled=True)]
    all_to_all x2 -> x3, waiting for transfers between devices: 19.9 us -> 83 us  [per_device(): lax.all_to_all(filtered, 'state', split_axis=0, concat_axis=0, tiled=True)]
    pallas_call x3, Pallas kernels: 30 us -> 34.3 us  [the longest x1 18.9 us: run_finish(): pl.pallas_call(functools.partial(finish_kernel, factor_scale), in_specs=[...]
    pallas_call x3, Pallas kernels: 71.3 us -> 74.7 us  [run_filter(): pl.pallas_call(filter_kernel, grid=(count,), in_specs=[pl.BlockSpec(memor...]
    all_to_all x2 -> x3, starting transfers between devices: 13.2 us -> 15.8 us  [per_device(): lax.all_to_all(filtered, 'state', split_axis=0, concat_axis=0, tiled=True)]
  transfers between devices with their start and end apart: 2 -> 3, of which waited for: 1 -> 3; matrix products, arithmetic and copies ran while one was open for 0% -> 0% of each run, Pallas kernels for 25% -> 27%
where the time goes in v3:
time: 237 us
  Pallas kernels  109 us (46%)
  waiting for transfers between devices  83 us (35%)
  blocking collectives  27.4 us (12%)
  starting transfers between devices  15.8 us (7%)
    all_to_all x3, waiting for transfers between devices, per_device(): lax.all_to_all(filtered, 'state', split_axis=0, concat_axis=0, tiled=True)  83 us
    pallas_call x3, Pallas kernels, run_filter(): pl.pallas_call(filter_kernel, grid=(count,), in_specs=[pl.BlockSpec(memor...  74.7 us
    all_to_all x2, blocking collectives, per_device(): lax.all_to_all(gram, 'state', split_axis=0, concat_axis=0, tiled=True)  27.4 us
    pallas_call x1, Pallas kernels, run_finish(): pl.pallas_call(functools.partial(finish_kernel, factor_scale), in_specs=[...  18.9 us
    all_to_all x3, starting transfers between devices, per_device(): lax.all_to_all(filtered, 'state', split_axis=0, concat_axis=0, tiled=True)  15.8 us
    pallas_call x1, Pallas kernels, run_gram(): pl.pallas_call(functools.partial(early_kernel, tall), grid=(rows // tall,...  8.15 us
    pallas_call x1, Pallas kernels, run_gram(): pl.pallas_call(functools.partial(late_kernel, tall), grid=(rows // tall,)...  7.28 us
  transfers between devices with their start and end apart: 3, of which 3 were waited for; matrix products, arithmetic and copies ran while one was open for 0% of the time, Pallas kernels for 27%

profile of v3, /device:TPU:0, one launch (start us, length us, event | category | flops | bytes accessed | tf_op | source)
XLA Modules:
  0.0 236.6 jit_solution(261616946540586982)
XLA Ops:
  0.0 19.2 %filter_0.1 = f32[32,2,48,128]{3,2,1,0:T(8,128)} custom-call(s32[2]{0:T(128)} %bounds.5, bf16[8,32,48,128]{3,2,1,0:T(8,128)(2,1)} %states.5, f32[32,48,128]{2,1,0:T(8,128)} %potential.5), custom_call_target="tpu_custom_call" | custom-call | flops 113246208 | bytes 3145728 | tf_op jit(solution)/shard_map/filter_0/pallas_call | solution.py:104
  19.2 7.3 %all-to-all-start = ((f32[32,2,48,128]{3,2,1,0:T(8,128)}), f32[32,2,48,128]{3,2,1,0:T(8,128)S(1)}, u32[]{:S(2)}, u32[]{:S(2)}) async-start(f32[32,2,48,128]{3,2,1,0:T(8,128)} %filter_0.1), calls=%async_computation | async-start | bytes 3145728 | tf_op jit(solution)/shard_map/all_to_all | solution.py:431
  26.5 36.2 %filter_2.1 = f32[32,4,48,128]{3,2,1,0:T(8,128)} custom-call(s32[2]{0:T(128)} %bounds.5, bf16[8,32,48,128]{3,2,1,0:T(8,128)(2,1)} %states.5, f32[32,48,128]{2,1,0:T(8,128)} %potential.5), custom_call_target="tpu_custom_call" | custom-call | flops 226492416 | bytes 5505024 | tf_op jit(solution)/shard_map/filter_2/pallas_call | solution.py:104
  62.7 1.5 all-to-all-done.refs_0_
  64.2 0.0 copy-start.1
  64.2 1.1 copy-done.1
  65.3 4.4 %all-to-all-start.1 = ((f32[32,4,48,128]{3,2,1,0:T(8,128)}), f32[32,4,48,128]{3,2,1,0:T(8,128)S(1)}, u32[]{:S(2)}, u32[]{:S(2)}) async-start(f32[32,4,48,128]{3,2,1,0:T(8,128)} %filter_2.1), calls=%async_computation.1 | async-start | bytes 6291456 | tf_op jit(solution)/shard_map/all_to_all | solution.py:431
  69.7 19.3 %filter_6.1 = f32[32,2,48,128]{3,2,1,0:T(8,128)} custom-call(s32[2]{0:T(128)} %bounds.5, bf16[8,32,48,128]{3,2,1,0:T(8,128)(2,1)} %states.5, f32[32,48,128]{2,1,0:T(8,128)} %potential.5), custom_call_target="tpu_custom_call" | custom-call | flops 113246208 | bytes 3145728 | tf_op jit(solution)/shard_map/filter_6/pallas_call | solution.py:104
  89.0 52.0 %all-to-all-done.1.refs_1_ = f32[32,4,48,128]{3,2,1,0:T(8,128)S(1)} async-done(((f32[32,4,48,128]{3,2,1,0:T(8,128)}), f32[32,4,48,128]{3,2,1,0:T(8,128)S(1)}, u32[]{:S(2)}, u32[]{:S(2)}) %all-to-all-start.1) | async-done | bytes 3145760 | tf_op jit(solution)/shard_map/all_to_all | solution.py:431
  141.0 0.0 copy-start
  141.0 4.1 %all-to-all-start.2 = ((f32[32,2,48,128]{3,2,1,0:T(8,128)}), f32[32,2,48,128]{3,2,1,0:T(8,128)}, u32[]{:S(2)}, u32[]{:S(2)}) async-start(f32[32,2,48,128]{3,2,1,0:T(8,128)} %filter_6.1), calls=%async_computation.2 | async-start | bytes 3145728 | tf_op jit(solution)/shard_map/all_to_all | solution.py:431
  145.2 0.0 copy-done
  145.2 8.1 %early_gram.1 = (bf16[192,6144]{1,0:T(8,128)(2,1)}, bf16[192,6144]{1,0:T(8,128)(2,1)}, f32[192,192]{1,0:T(8,128)}) custom-call(f32[32,2,48,128]{3,2,1,0:T(8,128)} %copy-done.1, f32[32,4,48,128]{3,2,1,0:T(8,128)} %copy-done), custom_call_target="tpu_custom_call" | custom-call | flops 905969664 | bytes 9437184 | tf_op jit(solution)/shard_map/early_gram/pallas_call | solution.py:233
  153.3 29.5 %all-to-all-done.2.piece = f32[32,2,48,128]{3,2,1,0:T(8,128)} async-done(((f32[32,2,48,128]{3,2,1,0:T(8,128)}), f32[32,2,48,128]{3,2,1,0:T(8,128)}, u32[]{:S(2)}, u32[]{:S(2)}) %all-to-all-start.2) | async-done | bytes 1572896 | tf_op jit(solution)/shard_map/all_to_all | solution.py:431
  182.8 7.3 %late_gram.1 = (bf16[64,6144]{1,0:T(8,128)(2,1)}, bf16[64,6144]{1,0:T(8,128)(2,1)}, f32[32,16,128]{2,1,0:T(8,128)}) custom-call(bf16[192,6144]{1,0:T(8,128)(2,1)} %get-tuple-element.11.early_high.refs_0_, bf16[192,6144]{1,0:T(8,128)(2,1)} %get-tuple-element.12.early_low.refs_1_, f32[192,192]{1,0:T(8,128)} %get-tuple-element.13.early_gram, ...), custom_call_target="tpu_custom_call" | custom-call | tf_op jit(solution)/shard_map/late_gram/pallas_call | solution.py:247
  190.1 14.4 %all_to_all.25 = f32[32,16,128]{2,1,0:T(8,128)S(1)} all-to-all(f32[32,16,128]{2,1,0:T(8,128)} %get-tuple-element.14), channel_id=1, replica_groups=mesh['cuts'=1,'state'=32] {'state'}, dimensions={0} | all-to-all | bytes 524288 | tf_op jit(solution)/shard_map/all_to_all | solution.py:434
  204.5 13.0 %all_to_all.26.gram = f32[32,16,128]{2,1,0:T(8,128)} all-to-all(f32[32,16,128]{2,1,0:T(8,128)S(1)} %broadcast_in_dim.2), channel_id=1, replica_groups=mesh['cuts'=1,'state'=32] {'state'}, dimensions={0} | all-to-all | bytes 524288 | tf_op jit(solution)/shard_map/all_to_all | solution.py:436
  217.5 18.9 %finish.1 = f32[256,6144]{1,0:T(8,128)} custom-call(f32[32,16,128]{2,1,0:T(8,128)} %all_to_all.26.gram, bf16[192,6144]{1,0:T(8,128)(2,1)} %get-tuple-element.11.early_high.refs_0_, bf16[192,6144]{1,0:T(8,128)(2,1)} %get-tuple-element.12.early_low.refs_1_, bf16[64,6144]{1,0:T(8,128)(2,1)} %get-tuple-element.15.refs_2_, bf16[64,6144]{1,0:T(8,128)(2,1)} %get-tuple-element.16.refs_3_), custom_call_target="tpu_custom_call" | custom-call | tf_op jit(solution)/shard_map/finish/pallas_call | solution.py:398
  (2 shorter events, 0.1 us)
Async XLA Ops:
  19.2 45.0 %all-to-all-start = ((f32[32,2,48,128]{3,2,1,0:T(8,128)}), f32[32,2,48,128]{3,2,1,0:T(8,128)S(1)}, u32[]{:S(2)}, u32[]{:S(2)}) async-start(f32[32,2,48,128]{3,2,1,0:T(8,128)} %filter_0.1), calls=%async_computation | async-start | bytes 3145728 | tf_op jit(solution)/shard_map/all_to_all | solution.py:431
  64.2 1.1 copy-start.1
  65.3 75.7 %all-to-all-start.1 = ((f32[32,4,48,128]{3,2,1,0:T(8,128)}), f32[32,4,48,128]{3,2,1,0:T(8,128)S(1)}, u32[]{:S(2)}, u32[]{:S(2)}) async-start(f32[32,4,48,128]{3,2,1,0:T(8,128)} %filter_2.1), calls=%async_computation.1 | async-start | bytes 6291456 | tf_op jit(solution)/shard_map/all_to_all | solution.py:431
  141.0 4.2 %copy-start = (f32[32,4,48,128]{3,2,1,0:T(8,128)}, f32[32,4,48,128]{3,2,1,0:T(8,128)S(1)}, u32[]{:S(2)}) copy-start(f32[32,4,48,128]{3,2,1,0:T(8,128)S(1)} %all-to-all-done.1.refs_1_) | copy-start | bytes 9437188
  141.0 41.8 %all-to-all-start.2 = ((f32[32,2,48,128]{3,2,1,0:T(8,128)}), f32[32,2,48,128]{3,2,1,0:T(8,128)}, u32[]{:S(2)}, u32[]{:S(2)}) async-start(f32[32,2,48,128]{3,2,1,0:T(8,128)} %filter_6.1), calls=%async_computation.2 | async-start | bytes 3145728 | tf_op jit(solution)/shard_map/all_to_all | solution.py:431

commit v4 on v3

--- a/solution.py
+++ b/solution.py
@@ -319,22 +319,27 @@
     ]
     for copy in copies:
         copy.start()
-    high, low = invert_factor(factor_scale, gram, work, turn)
-    both = jnp.concatenate([high, low], axis=0)
-    for copy in copies:
-        copy.wait()
-    size, wide = stage.shape[1:]
+    slots, height, wide = stage.shape
     sent = []
-    for t in range(out.shape[1] // wide):
-        columns = pl.ds(t * wide, wide)
-        main = dot(both, right[0, :, columns], ((1,), (0,)))
-        rest = dot(high, right[1, :, columns], ((1,), (0,)))
-        if t >= 2:
-            sent[t - 2].wait()
-        stage[t % 2] = main[:size] + (main[size:] + rest)
-        sent.append(pltpu.make_async_copy(stage.at[t % 2], out.at[:, columns], leave.at[t % 2]))
-        sent[t].start()
-    for copy in sent[-2:]:
+    for half, (high, low) in enumerate(invert_factor(factor_scale, gram, work, turn)):
+        if half == 0:
+            for copy in copies:
+                copy.wait()
+        both = jnp.concatenate([high, low], axis=0)
+        lines = pl.ds(half * height, height)
+        for t in range(out.shape[1] // wide):
+            columns = pl.ds(t * wide, wide)
+            main = dot(both, right[0, :, columns], ((1,), (0,)))
+            rest = dot(high, right[1, :, columns], ((1,), (0,)))
+            slot = len(sent) % slots
+            if len(sent) >= slots:
+                sent[len(sent) - slots].wait()
+            stage[slot] = main[:height] + (main[height:] + rest)
+            sent.append(
+                pltpu.make_async_copy(stage.at[slot], out.at[lines, columns], leave.at[slot])
+            )
+            sent[-1].start()
+    for copy in sent[-slots:]:
         copy.wait()
 
 
@@ -368,16 +373,14 @@
         if k + BLOCK < size:
             below = panel[:, k + BLOCK : size]
             work[k + BLOCK :, :] -= exact_dot(below, panel, ((0,), (0,)))
-    mixed = (work[:, size:] * factor_scale).T
-    for k in range(halves):
-        turn[k] = mixed[:, k * LANES : (k + 1) * LANES]
-    columns = [
-        jnp.concatenate(
-            [turn[k, pl.ds(c, sources, stride=per_device), :] for c in range(per_device)], axis=0
-        )
-        for k in range(halves)
-    ]
-    return split(jnp.concatenate(columns, axis=1).T)
+        if (k + BLOCK) % LANES == 0:
+            half = k // LANES
+            final = work[half * LANES : (half + 1) * LANES, size:] * factor_scale
+            turn[half] = final.T
+            parts = [
+                turn[half, pl.ds(c, sources, stride=per_device), :] for c in range(per_device)
+            ]
+            yield split(jnp.concatenate(parts, axis=0).T)
 
 
 def to_states(whole, sources, turn):
@@ -404,9 +407,9 @@
             pltpu.VMEM((size, 2 * size), jnp.float32),
             pltpu.VMEM((size // LANES, size, LANES), jnp.float32),
             pltpu.VMEM((2, size, points), jnp.bfloat16),
-            pltpu.VMEM((2, size, wide), jnp.float32),
+            pltpu.VMEM((points // wide, LANES, wide), jnp.float32),
             pltpu.SemaphoreType.DMA((len(rows),)),
-            pltpu.SemaphoreType.DMA((2,)),
+            pltpu.SemaphoreType.DMA((points // wide,)),
         ],
         name="finish",
     )(gram, *rows)

time: 237 us -> 236 us (level)
  no operation moved by 1% of the time
where the time goes in v4:
time: 236 us
  Pallas kernels  108 us (46%)
  waiting for transfers between devices  83 us (35%)
  blocking collectives  27.4 us (12%)
  starting transfers between devices  15.8 us (7%)
    all_to_all x3, waiting for transfers between devices, per_device(): lax.all_to_all(filtered, 'state', split_axis=0, concat_axis=0, tiled=True)  83 us
    pallas_call x3, Pallas kernels, run_filter(): pl.pallas_call(filter_kernel, grid=(count,), in_specs=[pl.BlockSpec(memor...  74.7 us
    all_to_all x2, blocking collectives, per_device(): lax.all_to_all(gram, 'state', split_axis=0, concat_axis=0, tiled=True)  27.4 us
    pallas_call x1, Pallas kernels, run_finish(): pl.pallas_call(functools.partial(finish_kernel, factor_scale), in_specs=[...  18.1 us
    all_to_all x3, starting transfers between devices, per_device(): lax.all_to_all(filtered, 'state', split_axis=0, concat_axis=0, tiled=True)  15.8 us
    pallas_call x1, Pallas kernels, run_gram(): pl.pallas_call(functools.partial(early_kernel, tall), grid=(rows // tall,...  8.15 us
    pallas_call x1, Pallas kernels, run_gram(): pl.pallas_call(functools.partial(late_kernel, tall), grid=(rows // tall,)...  7.28 us
  transfers between devices with their start and end apart: 3, of which 3 were waited for; matrix products, arithmetic and copies ran while one was open for 0% of the time, Pallas kernels for 27%

profile of v4, /device:TPU:0, one launch (start us, length us, event | category | flops | bytes accessed | tf_op | source)
XLA Modules:
  0.0 235.8 jit_solution(2806076924528610007)
XLA Ops:
  0.0 19.2 %filter_0.1 = f32[32,2,48,128]{3,2,1,0:T(8,128)} custom-call(s32[2]{0:T(128)} %bounds.5, bf16[8,32,48,128]{3,2,1,0:T(8,128)(2,1)} %states.5, f32[32,48,128]{2,1,0:T(8,128)} %potential.5), custom_call_target="tpu_custom_call" | custom-call | flops 113246208 | bytes 3145728 | tf_op jit(solution)/shard_map/filter_0/pallas_call | solution.py:104
  19.2 7.3 %all-to-all-start = ((f32[32,2,48,128]{3,2,1,0:T(8,128)}), f32[32,2,48,128]{3,2,1,0:T(8,128)S(1)}, u32[]{:S(2)}, u32[]{:S(2)}) async-start(f32[32,2,48,128]{3,2,1,0:T(8,128)} %filter_0.1), calls=%async_computation | async-start | bytes 3145728 | tf_op jit(solution)/shard_map/all_to_all | solution.py:434
  26.5 36.2 %filter_2.1 = f32[32,4,48,128]{3,2,1,0:T(8,128)} custom-call(s32[2]{0:T(128)} %bounds.5, bf16[8,32,48,128]{3,2,1,0:T(8,128)(2,1)} %states.5, f32[32,48,128]{2,1,0:T(8,128)} %potential.5), custom_call_target="tpu_custom_call" | custom-call | flops 226492416 | bytes 5505024 | tf_op jit(solution)/shard_map/filter_2/pallas_call | solution.py:104
  62.7 1.5 all-to-all-done.refs_0_
  64.2 0.0 copy-start.1
  64.2 1.1 copy-done.1
  65.3 4.4 %all-to-all-start.1 = ((f32[32,4,48,128]{3,2,1,0:T(8,128)}), f32[32,4,48,128]{3,2,1,0:T(8,128)S(1)}, u32[]{:S(2)}, u32[]{:S(2)}) async-start(f32[32,4,48,128]{3,2,1,0:T(8,128)} %filter_2.1), calls=%async_computation.1 | async-start | bytes 6291456 | tf_op jit(solution)/shard_map/all_to_all | solution.py:434
  69.7 19.3 %filter_6.1 = f32[32,2,48,128]{3,2,1,0:T(8,128)} custom-call(s32[2]{0:T(128)} %bounds.5, bf16[8,32,48,128]{3,2,1,0:T(8,128)(2,1)} %states.5, f32[32,48,128]{2,1,0:T(8,128)} %potential.5), custom_call_target="tpu_custom_call" | custom-call | flops 113246208 | bytes 3145728 | tf_op jit(solution)/shard_map/filter_6/pallas_call | solution.py:104
  89.0 52.0 %all-to-all-done.1.refs_1_ = f32[32,4,48,128]{3,2,1,0:T(8,128)S(1)} async-done(((f32[32,4,48,128]{3,2,1,0:T(8,128)}), f32[32,4,48,128]{3,2,1,0:T(8,128)S(1)}, u32[]{:S(2)}, u32[]{:S(2)}) %all-to-all-start.1) | async-done | bytes 3145760 | tf_op jit(solution)/shard_map/all_to_all | solution.py:434
  141.0 0.0 copy-start
  141.0 4.1 %all-to-all-start.2 = ((f32[32,2,48,128]{3,2,1,0:T(8,128)}), f32[32,2,48,128]{3,2,1,0:T(8,128)}, u32[]{:S(2)}, u32[]{:S(2)}) async-start(f32[32,2,48,128]{3,2,1,0:T(8,128)} %filter_6.1), calls=%async_computation.2 | async-start | bytes 3145728 | tf_op jit(solution)/shard_map/all_to_all | solution.py:434
  145.2 0.0 copy-done
  145.2 8.1 %early_gram.1 = (bf16[192,6144]{1,0:T(8,128)(2,1)}, bf16[192,6144]{1,0:T(8,128)(2,1)}, f32[192,192]{1,0:T(8,128)}) custom-call(f32[32,2,48,128]{3,2,1,0:T(8,128)} %copy-done.1, f32[32,4,48,128]{3,2,1,0:T(8,128)} %copy-done), custom_call_target="tpu_custom_call" | custom-call | flops 905969664 | bytes 9437184 | tf_op jit(solution)/shard_map/early_gram/pallas_call | solution.py:233
  153.3 29.5 %all-to-all-done.2.piece = f32[32,2,48,128]{3,2,1,0:T(8,128)} async-done(((f32[32,2,48,128]{3,2,1,0:T(8,128)}), f32[32,2,48,128]{3,2,1,0:T(8,128)}, u32[]{:S(2)}, u32[]{:S(2)}) %all-to-all-start.2) | async-done | bytes 1572896 | tf_op jit(solution)/shard_map/all_to_all | solution.py:434
  182.8 7.3 %late_gram.1 = (bf16[64,6144]{1,0:T(8,128)(2,1)}, bf16[64,6144]{1,0:T(8,128)(2,1)}, f32[32,16,128]{2,1,0:T(8,128)}) custom-call(bf16[192,6144]{1,0:T(8,128)(2,1)} %get-tuple-element.11.early_high.refs_0_, bf16[192,6144]{1,0:T(8,128)(2,1)} %get-tuple-element.12.early_low.refs_1_, f32[192,192]{1,0:T(8,128)} %get-tuple-element.13.early_gram, ...), custom_call_target="tpu_custom_call" | custom-call | tf_op jit(solution)/shard_map/late_gram/pallas_call | solution.py:247
  190.1 14.4 %all_to_all.25 = f32[32,16,128]{2,1,0:T(8,128)S(1)} all-to-all(f32[32,16,128]{2,1,0:T(8,128)} %get-tuple-element.14), channel_id=1, replica_groups=mesh['cuts'=1,'state'=32] {'state'}, dimensions={0} | all-to-all | bytes 524288 | tf_op jit(solution)/shard_map/all_to_all | solution.py:437
  204.5 13.0 %all_to_all.26.gram = f32[32,16,128]{2,1,0:T(8,128)} all-to-all(f32[32,16,128]{2,1,0:T(8,128)S(1)} %broadcast_in_dim.2), channel_id=1, replica_groups=mesh['cuts'=1,'state'=32] {'state'}, dimensions={0} | all-to-all | bytes 524288 | tf_op jit(solution)/shard_map/all_to_all | solution.py:439
  217.5 18.1 %finish.1 = f32[256,6144]{1,0:T(8,128)} custom-call(f32[32,16,128]{2,1,0:T(8,128)} %all_to_all.26.gram, bf16[192,6144]{1,0:T(8,128)(2,1)} %get-tuple-element.11.early_high.refs_0_, bf16[192,6144]{1,0:T(8,128)(2,1)} %get-tuple-element.12.early_low.refs_1_, bf16[64,6144]{1,0:T(8,128)(2,1)} %get-tuple-element.15.refs_2_, bf16[64,6144]{1,0:T(8,128)(2,1)} %get-tuple-element.16.refs_3_), custom_call_target="tpu_custom_call" | custom-call | tf_op jit(solution)/shard_map/finish/pallas_call | solution.py:401
  (2 shorter events, 0.1 us)
Async XLA Ops:
  19.2 45.0 %all-to-all-start = ((f32[32,2,48,128]{3,2,1,0:T(8,128)}), f32[32,2,48,128]{3,2,1,0:T(8,128)S(1)}, u32[]{:S(2)}, u32[]{:S(2)}) async-start(f32[32,2,48,128]{3,2,1,0:T(8,128)} %filter_0.1), calls=%async_computation | async-start | bytes 3145728 | tf_op jit(solution)/shard_map/all_to_all | solution.py:434
  64.2 1.1 copy-start.1
  65.3 75.7 %all-to-all-start.1 = ((f32[32,4,48,128]{3,2,1,0:T(8,128)}), f32[32,4,48,128]{3,2,1,0:T(8,128)S(1)}, u32[]{:S(2)}, u32[]{:S(2)}) async-start(f32[32,4,48,128]{3,2,1,0:T(8,128)} %filter_2.1), calls=%async_computation.1 | async-start | bytes 6291456 | tf_op jit(solution)/shard_map/all_to_all | solution.py:434
  141.0 4.2 %copy-start = (f32[32,4,48,128]{3,2,1,0:T(8,128)}, f32[32,4,48,128]{3,2,1,0:T(8,128)S(1)}, u32[]{:S(2)}) copy-start(f32[32,4,48,128]{3,2,1,0:T(8,128)S(1)} %all-to-all-done.1.refs_1_) | copy-start | bytes 9437188
  141.0 41.8 %all-to-all-start.2 = ((f32[32,2,48,128]{3,2,1,0:T(8,128)}), f32[32,2,48,128]{3,2,1,0:T(8,128)}, u32[]{:S(2)}, u32[]{:S(2)}) async-start(f32[32,2,48,128]{3,2,1,0:T(8,128)} %filter_6.1), calls=%async_computation.2 | async-start | bytes 3145728 | tf_op jit(solution)/shard_map/all_to_all | solution.py:434
